TPU v7x, 32 devices: a whole 2x2x4 slice. The times are simulated.
32 devices in a mesh: space: 16 (over z, x, core), ens: 2 (over y).
Axes of the slice: x: 2, y: 2, z: 4, core: 2. Of those that a mesh axis runs over, the one named last changes fastest.
Arguments:
- params: float32 [64, 256, 512], P('ens', 'space'), may hold values from 0.55 to 0.8
- base_thickness: float32 [256, 512], P('space'), may hold values from 0.5 to 3
- balance: float32 [256, 512], P('space'), may hold values from -0.1 to 0.3
- step_count: int32 [64], replicated, may hold values from 8 to 32, as said below
- obs_index: int32 [4096], P('space'), may hold values from 0 to 8191
- observed: float32 [4096], P('space'), may hold values from 0.5 to 2
- noise_var: float32 [4096], P('space'), may hold values from 0.5 to 4
Outputs:
- thickness: float32 [64, 256, 512], P('ens', 'space')
- updated: float32 [64, 256, 512], P('ens', 'space')
Inputs may be any that keep to these rules, and one draw needn't show every extreme that they name: `step_count`: some member runs exactly 32 steps.
All inputs are finite; a program needn't handle non-finite values.
Results may differ from a plain program's by a relative error of at most 0.000074.
Values sent between devices are 32-bit elements; how exact they have to be, the bound alone decides.
A program may use at most 64 MiB of HBM per device.

v0:
```python
import jax
import jax.numpy as jnp
from jax import lax
from jax.sharding import PartitionSpec as P

time_step = 0.11


def padded_2(block, sides, width):
    for axis, dim in sides:
        count = lax.axis_size(axis)
        forward = [(i, i + 1) for i in range(count - 1)]
        backward = [(target, source) for source, target in forward]
        low = lax.ppermute(
            lax.slice_in_dim(block, block.shape[dim] - width, None, axis=dim), axis, forward
        )
        high = lax.ppermute(lax.slice_in_dim(block, 0, width, axis=dim), axis, backward)
        block = jnp.concatenate([low, block, high], axis=dim)
    return block


def stencil(padded, slip_padded, thickness, balance):
    diffusivity = slip_padded * padded * padded / (1.0 + padded * padded)
    centre = diffusivity[:, 1:-1, 1:-1]
    divergence = jnp.zeros_like(thickness)
    for row_part, col_part in (
        (slice(2, None), slice(1, -1)),
        (slice(None, -2), slice(1, -1)),
        (slice(1, -1), slice(2, None)),
        (slice(1, -1), slice(None, -2)),
    ):
        divergence = divergence + 0.5 * (diffusivity[:, row_part, col_part] + centre) * (
            padded[:, row_part, col_part] - thickness
        )
    return thickness + time_step * (divergence + balance)


def ensemble_terms(predicted, observed, noise_var):
    members = predicted.shape[0]
    scaling = lax.rsqrt(noise_var)
    average = jnp.mean(predicted, axis=0)
    anomalies = (predicted - average) * scaling / jnp.sqrt(jnp.float32(members - 1))
    mismatch = (observed - predicted) * scaling
    gram = jnp.dot(anomalies, anomalies.T, precision=lax.Precision.HIGHEST)
    cross = jnp.dot(anomalies, mismatch.T, precision=lax.Precision.HIGHEST)
    return (gram, cross)


def solve_weights(gram, cross):
    members = gram.shape[0]
    factor = jnp.linalg.cholesky(gram + jnp.eye(members, dtype=gram.dtype))
    inner = lax.linalg.triangular_solve(factor, cross, left_side=True, lower=True)
    result = lax.linalg.triangular_solve(
        factor, inner, left_side=True, lower=True, transpose_a=True
    )
    return result / jnp.sqrt(jnp.float32(members - 1))


def shards(params, base_thickness, balance, step_count, obs_index, observed, noise_var):
    members_dev = params.shape[0]
    ens_index = lax.axis_index("ens")
    members = members_dev * lax.axis_size("ens")
    own_counts = lax.dynamic_slice_in_dim(step_count, ens_index * members_dev, members_dev)
    longest = jnp.max(own_counts)
    initial = jnp.broadcast_to(base_thickness[None], params.shape)
    slip_rows = padded_2(jnp.exp(params), (("space", 1),), 1)
    slip_padded = jnp.pad(slip_rows, ((0, 0), (0, 0), (1, 1)))

    def advance(step_index, thickness):
        rimmed = padded_2(thickness, (("space", 1),), 1)
        padded = jnp.pad(rimmed, ((0, 0), (0, 0), (1, 1)))
        moved = stencil(padded, slip_padded, thickness, balance)
        return jnp.where((step_index < own_counts)[:, None, None], moved, thickness)

    thickness = lax.fori_loop(0, longest, advance, initial)
    tile_cells = params.shape[1] * params.shape[2]
    predicted = jnp.take(thickness.reshape(members_dev, tile_cells), obs_index, axis=1)
    obs_block = lax.all_to_all(predicted, "ens", split_axis=1, concat_axis=0, tiled=True)
    block_width = obs_block.shape[1]
    observed_part = lax.dynamic_slice_in_dim(observed, ens_index * block_width, block_width)
    noise_part = lax.dynamic_slice_in_dim(noise_var, ens_index * block_width, block_width)
    gram, cross = ensemble_terms(obs_block, observed_part, noise_part)
    gram, cross = lax.psum((gram, cross), ("space", "ens"))
    weights = solve_weights(gram, cross)
    weight_cols = lax.dynamic_slice_in_dim(weights, ens_index * members_dev, members_dev, 1)
    piece = lax.all_gather(params, "ens", axis=0, tiled=True)
    piece_rows = piece.shape[0]
    flat_piece = piece.reshape(piece_rows, tile_cells)
    weighted = jnp.dot(weight_cols.T, flat_piece, precision=lax.Precision.HIGHEST)
    weighted, member_total = (weighted, jnp.sum(flat_piece, axis=0))
    column_sums = jnp.sum(weight_cols, axis=0)
    increment = weighted - column_sums[:, None] * member_total[None, :] / members
    updated = params + increment.reshape(params.shape)
    return (thickness, updated)


def solution(mesh):
    in_specs = (
        P("ens", "space", None),
        P("space", None),
        P("space", None),
        P(),
        P("space"),
        P("space"),
        P("space"),
    )
    out_specs = (P("ens", "space", None), P("ens", "space", None))
    return jax.shard_map(shards, mesh=mesh, in_specs=in_specs, out_specs=out_specs, check_vma=False)
```

profile of v0, /device:TPU:0, one launch (start us, length us, event | category | flops | bytes accessed | tf_op | source)
XLA Modules:
  0.0 560.8 jit_solution(4297953380214112374)
XLA Ops:
  14.0 3.1 collective-permute-done.3
  19.3 447.2 %while.12 = (s32[]{:T(128)}, f32[32,16,512]{2,1,0:T(8,128)}, s32[]{:T(128)}, s32[32]{0:T(128)S(1)}, f32[32,18,514]{2,1,0:T(8,128)S(1)}, /*index=5*/f32[16,512]{1,0:T(8,128)S(1)}, s32[]{:T(128)}) while((s32[]{:T(128)}, f32[32,16,512]{2,1,0:T(8,128)}, s32[]{:T(128)}, s32[32]{0:T(128)S(1)}, f32[32,18,514]{2,1,0:T(8,128)S(1)}, ...), condition=%wide.region_2.3_spmd, body=%wide.region_1.2_spmd.sunk | while | flops 10402466 | bytes 17217376 | solution.py:75
  22.6 5.4 collective-permute-start.1
  35.9 5.3 collective-permute-start.1
  49.1 6.0 %collective-permute-start.1 = (f32[32,1,512]{2,1,0:T(1,128)S(1)}, f32[32,1,512]{2,1,0:T(1,128)S(1)}, u32[]{:S(2)}, u32[]{:S(2)}) collective-permute-start(f32[32,1,512]{2,1,0:T(1,128)S(1)} %get-tuple-element.150), channel_id=1, source_target_pairs={{0,2},{2,4},{4,6},{6,8},{8,10},{10,12},{12,14},{14,16},{16,18},{18... | collective-permute-start | bytes 196616 | tf_op jit(solution)/shard_map/while/body/ppermute | solution.py:14
  57.1 2.7 add_select_fusion.2
  63.0 5.4 collective-permute-start.1
  70.4 2.7 add_select_fusion.2
  76.4 6.0 %collective-permute-start.1 = (f32[32,1,512]{2,1,0:T(1,128)S(1)}, f32[32,1,512]{2,1,0:T(1,128)S(1)}, u32[]{:S(2)}, u32[]{:S(2)}) collective-permute-start(f32[32,1,512]{2,1,0:T(1,128)S(1)} %get-tuple-element.150), channel_id=1, source_target_pairs={{0,2},{2,4},{4,6},{6,8},{8,10},{10,12},{12,14},{14,16},{16,18},{18... | collective-permute-start | bytes 196616 | tf_op jit(solution)/shard_map/while/body/ppermute | solution.py:14
  90.3 6.0 %collective-permute-start.1 = (f32[32,1,512]{2,1,0:T(1,128)S(1)}, f32[32,1,512]{2,1,0:T(1,128)S(1)}, u32[]{:S(2)}, u32[]{:S(2)}) collective-permute-start(f32[32,1,512]{2,1,0:T(1,128)S(1)} %get-tuple-element.150), channel_id=1, source_target_pairs={{0,2},{2,4},{4,6},{6,8},{8,10},{10,12},{12,14},{14,16},{16,18},{18... | collective-permute-start | bytes 196616 | tf_op jit(solution)/shard_map/while/body/ppermute | solution.py:14
  104.3 5.3 collective-permute-start.1
  111.5 2.7 add_select_fusion.2
  117.5 5.3 collective-permute-start.1
  124.8 2.7 add_select_fusion.2
  130.8 5.3 collective-permute-start.1
  138.0 2.7 add_select_fusion.2
  144.0 6.2 %collective-permute-start.1 = (f32[32,1,512]{2,1,0:T(1,128)S(1)}, f32[32,1,512]{2,1,0:T(1,128)S(1)}, u32[]{:S(2)}, u32[]{:S(2)}) collective-permute-start(f32[32,1,512]{2,1,0:T(1,128)S(1)} %get-tuple-element.150), channel_id=1, source_target_pairs={{0,2},{2,4},{4,6},{6,8},{8,10},{10,12},{12,14},{14,16},{16,18},{18... | collective-permute-start | bytes 196616 | tf_op jit(solution)/shard_map/while/body/ppermute | solution.py:14
  158.2 6.2 %collective-permute-start.1 = (f32[32,1,512]{2,1,0:T(1,128)S(1)}, f32[32,1,512]{2,1,0:T(1,128)S(1)}, u32[]{:S(2)}, u32[]{:S(2)}) collective-permute-start(f32[32,1,512]{2,1,0:T(1,128)S(1)} %get-tuple-element.150), channel_id=1, source_target_pairs={{0,2},{2,4},{4,6},{6,8},{8,10},{10,12},{12,14},{14,16},{16,18},{18... | collective-permute-start | bytes 196616 | tf_op jit(solution)/shard_map/while/body/ppermute | solution.py:14
  172.3 6.2 %collective-permute-start.1 = (f32[32,1,512]{2,1,0:T(1,128)S(1)}, f32[32,1,512]{2,1,0:T(1,128)S(1)}, u32[]{:S(2)}, u32[]{:S(2)}) collective-permute-start(f32[32,1,512]{2,1,0:T(1,128)S(1)} %get-tuple-element.150), channel_id=1, source_target_pairs={{0,2},{2,4},{4,6},{6,8},{8,10},{10,12},{12,14},{14,16},{16,18},{18... | collective-permute-start | bytes 196616 | tf_op jit(solution)/shard_map/while/body/ppermute | solution.py:14
  186.4 6.2 %collective-permute-start.1 = (f32[32,1,512]{2,1,0:T(1,128)S(1)}, f32[32,1,512]{2,1,0:T(1,128)S(1)}, u32[]{:S(2)}, u32[]{:S(2)}) collective-permute-start(f32[32,1,512]{2,1,0:T(1,128)S(1)} %get-tuple-element.150), channel_id=1, source_target_pairs={{0,2},{2,4},{4,6},{6,8},{8,10},{10,12},{12,14},{14,16},{16,18},{18... | collective-permute-start | bytes 196616 | tf_op jit(solution)/shard_map/while/body/ppermute | solution.py:14
  200.6 6.2 %collective-permute-start.1 = (f32[32,1,512]{2,1,0:T(1,128)S(1)}, f32[32,1,512]{2,1,0:T(1,128)S(1)}, u32[]{:S(2)}, u32[]{:S(2)}) collective-permute-start(f32[32,1,512]{2,1,0:T(1,128)S(1)} %get-tuple-element.150), channel_id=1, source_target_pairs={{0,2},{2,4},{4,6},{6,8},{8,10},{10,12},{12,14},{14,16},{16,18},{18... | collective-permute-start | bytes 196616 | tf_op jit(solution)/shard_map/while/body/ppermute | solution.py:14
  214.7 6.2 %collective-permute-start.1 = (f32[32,1,512]{2,1,0:T(1,128)S(1)}, f32[32,1,512]{2,1,0:T(1,128)S(1)}, u32[]{:S(2)}, u32[]{:S(2)}) collective-permute-start(f32[32,1,512]{2,1,0:T(1,128)S(1)} %get-tuple-element.150), channel_id=1, source_target_pairs={{0,2},{2,4},{4,6},{6,8},{8,10},{10,12},{12,14},{14,16},{16,18},{18... | collective-permute-start | bytes 196616 | tf_op jit(solution)/shard_map/while/body/ppermute | solution.py:14
  228.8 6.2 %collective-permute-start.1 = (f32[32,1,512]{2,1,0:T(1,128)S(1)}, f32[32,1,512]{2,1,0:T(1,128)S(1)}, u32[]{:S(2)}, u32[]{:S(2)}) collective-permute-start(f32[32,1,512]{2,1,0:T(1,128)S(1)} %get-tuple-element.150), channel_id=1, source_target_pairs={{0,2},{2,4},{4,6},{6,8},{8,10},{10,12},{12,14},{14,16},{16,18},{18... | collective-permute-start | bytes 196616 | tf_op jit(solution)/shard_map/while/body/ppermute | solution.py:14
  243.0 6.2 %collective-permute-start.1 = (f32[32,1,512]{2,1,0:T(1,128)S(1)}, f32[32,1,512]{2,1,0:T(1,128)S(1)}, u32[]{:S(2)}, u32[]{:S(2)}) collective-permute-start(f32[32,1,512]{2,1,0:T(1,128)S(1)} %get-tuple-element.150), channel_id=1, source_target_pairs={{0,2},{2,4},{4,6},{6,8},{8,10},{10,12},{12,14},{14,16},{16,18},{18... | collective-permute-start | bytes 196616 | tf_op jit(solution)/shard_map/while/body/ppermute | solution.py:14
  257.1 6.2 %collective-permute-start.1 = (f32[32,1,512]{2,1,0:T(1,128)S(1)}, f32[32,1,512]{2,1,0:T(1,128)S(1)}, u32[]{:S(2)}, u32[]{:S(2)}) collective-permute-start(f32[32,1,512]{2,1,0:T(1,128)S(1)} %get-tuple-element.150), channel_id=1, source_target_pairs={{0,2},{2,4},{4,6},{6,8},{8,10},{10,12},{12,14},{14,16},{16,18},{18... | collective-permute-start | bytes 196616 | tf_op jit(solution)/shard_map/while/body/ppermute | solution.py:14
  271.2 6.2 %collective-permute-start.1 = (f32[32,1,512]{2,1,0:T(1,128)S(1)}, f32[32,1,512]{2,1,0:T(1,128)S(1)}, u32[]{:S(2)}, u32[]{:S(2)}) collective-permute-start(f32[32,1,512]{2,1,0:T(1,128)S(1)} %get-tuple-element.150), channel_id=1, source_target_pairs={{0,2},{2,4},{4,6},{6,8},{8,10},{10,12},{12,14},{14,16},{16,18},{18... | collective-permute-start | bytes 196616 | tf_op jit(solution)/shard_map/while/body/ppermute | solution.py:14
  285.4 6.2 %collective-permute-start.1 = (f32[32,1,512]{2,1,0:T(1,128)S(1)}, f32[32,1,512]{2,1,0:T(1,128)S(1)}, u32[]{:S(2)}, u32[]{:S(2)}) collective-permute-start(f32[32,1,512]{2,1,0:T(1,128)S(1)} %get-tuple-element.150), channel_id=1, source_target_pairs={{0,2},{2,4},{4,6},{6,8},{8,10},{10,12},{12,14},{14,16},{16,18},{18... | collective-permute-start | bytes 196616 | tf_op jit(solution)/shard_map/while/body/ppermute | solution.py:14
  299.5 6.2 %collective-permute-start.1 = (f32[32,1,512]{2,1,0:T(1,128)S(1)}, f32[32,1,512]{2,1,0:T(1,128)S(1)}, u32[]{:S(2)}, u32[]{:S(2)}) collective-permute-start(f32[32,1,512]{2,1,0:T(1,128)S(1)} %get-tuple-element.150), channel_id=1, source_target_pairs={{0,2},{2,4},{4,6},{6,8},{8,10},{10,12},{12,14},{14,16},{16,18},{18... | collective-permute-start | bytes 196616 | tf_op jit(solution)/shard_map/while/body/ppermute | solution.py:14
  313.6 6.2 %collective-permute-start.1 = (f32[32,1,512]{2,1,0:T(1,128)S(1)}, f32[32,1,512]{2,1,0:T(1,128)S(1)}, u32[]{:S(2)}, u32[]{:S(2)}) collective-permute-start(f32[32,1,512]{2,1,0:T(1,128)S(1)} %get-tuple-element.150), channel_id=1, source_target_pairs={{0,2},{2,4},{4,6},{6,8},{8,10},{10,12},{12,14},{14,16},{16,18},{18... | collective-permute-start | bytes 196616 | tf_op jit(solution)/shard_map/while/body/ppermute | solution.py:14
  327.8 6.2 %collective-permute-start.1 = (f32[32,1,512]{2,1,0:T(1,128)S(1)}, f32[32,1,512]{2,1,0:T(1,128)S(1)}, u32[]{:S(2)}, u32[]{:S(2)}) collective-permute-start(f32[32,1,512]{2,1,0:T(1,128)S(1)} %get-tuple-element.150), channel_id=1, source_target_pairs={{0,2},{2,4},{4,6},{6,8},{8,10},{10,12},{12,14},{14,16},{16,18},{18... | collective-permute-start | bytes 196616 | tf_op jit(solution)/shard_map/while/body/ppermute | solution.py:14
  341.9 6.2 %collective-permute-start.1 = (f32[32,1,512]{2,1,0:T(1,128)S(1)}, f32[32,1,512]{2,1,0:T(1,128)S(1)}, u32[]{:S(2)}, u32[]{:S(2)}) collective-permute-start(f32[32,1,512]{2,1,0:T(1,128)S(1)} %get-tuple-element.150), channel_id=1, source_target_pairs={{0,2},{2,4},{4,6},{6,8},{8,10},{10,12},{12,14},{14,16},{16,18},{18... | collective-permute-start | bytes 196616 | tf_op jit(solution)/shard_map/while/body/ppermute | solution.py:14
  356.1 6.2 %collective-permute-start.1 = (f32[32,1,512]{2,1,0:T(1,128)S(1)}, f32[32,1,512]{2,1,0:T(1,128)S(1)}, u32[]{:S(2)}, u32[]{:S(2)}) collective-permute-start(f32[32,1,512]{2,1,0:T(1,128)S(1)} %get-tuple-element.150), channel_id=1, source_target_pairs={{0,2},{2,4},{4,6},{6,8},{8,10},{10,12},{12,14},{14,16},{16,18},{18... | collective-permute-start | bytes 196616 | tf_op jit(solution)/shard_map/while/body/ppermute | solution.py:14
  370.2 6.2 %collective-permute-start.1 = (f32[32,1,512]{2,1,0:T(1,128)S(1)}, f32[32,1,512]{2,1,0:T(1,128)S(1)}, u32[]{:S(2)}, u32[]{:S(2)}) collective-permute-start(f32[32,1,512]{2,1,0:T(1,128)S(1)} %get-tuple-element.150), channel_id=1, source_target_pairs={{0,2},{2,4},{4,6},{6,8},{8,10},{10,12},{12,14},{14,16},{16,18},{18... | collective-permute-start | bytes 196616 | tf_op jit(solution)/shard_map/while/body/ppermute | solution.py:14
  384.3 6.2 %collective-permute-start.1 = (f32[32,1,512]{2,1,0:T(1,128)S(1)}, f32[32,1,512]{2,1,0:T(1,128)S(1)}, u32[]{:S(2)}, u32[]{:S(2)}) collective-permute-start(f32[32,1,512]{2,1,0:T(1,128)S(1)} %get-tuple-element.150), channel_id=1, source_target_pairs={{0,2},{2,4},{4,6},{6,8},{8,10},{10,12},{12,14},{14,16},{16,18},{18... | collective-permute-start | bytes 196616 | tf_op jit(solution)/shard_map/while/body/ppermute | solution.py:14
  398.5 6.2 %collective-permute-start.1 = (f32[32,1,512]{2,1,0:T(1,128)S(1)}, f32[32,1,512]{2,1,0:T(1,128)S(1)}, u32[]{:S(2)}, u32[]{:S(2)}) collective-permute-start(f32[32,1,512]{2,1,0:T(1,128)S(1)} %get-tuple-element.150), channel_id=1, source_target_pairs={{0,2},{2,4},{4,6},{6,8},{8,10},{10,12},{12,14},{14,16},{16,18},{18... | collective-permute-start | bytes 196616 | tf_op jit(solution)/shard_map/while/body/ppermute | solution.py:14
  412.6 6.2 %collective-permute-start.1 = (f32[32,1,512]{2,1,0:T(1,128)S(1)}, f32[32,1,512]{2,1,0:T(1,128)S(1)}, u32[]{:S(2)}, u32[]{:S(2)}) collective-permute-start(f32[32,1,512]{2,1,0:T(1,128)S(1)} %get-tuple-element.150), channel_id=1, source_target_pairs={{0,2},{2,4},{4,6},{6,8},{8,10},{10,12},{12,14},{14,16},{16,18},{18... | collective-permute-start | bytes 196616 | tf_op jit(solution)/shard_map/while/body/ppermute | solution.py:14
  426.7 6.2 %collective-permute-start.1 = (f32[32,1,512]{2,1,0:T(1,128)S(1)}, f32[32,1,512]{2,1,0:T(1,128)S(1)}, u32[]{:S(2)}, u32[]{:S(2)}) collective-permute-start(f32[32,1,512]{2,1,0:T(1,128)S(1)} %get-tuple-element.150), channel_id=1, source_target_pairs={{0,2},{2,4},{4,6},{6,8},{8,10},{10,12},{12,14},{14,16},{16,18},{18... | collective-permute-start | bytes 196616 | tf_op jit(solution)/shard_map/while/body/ppermute | solution.py:14
  440.9 6.2 %collective-permute-start.1 = (f32[32,1,512]{2,1,0:T(1,128)S(1)}, f32[32,1,512]{2,1,0:T(1,128)S(1)}, u32[]{:S(2)}, u32[]{:S(2)}) collective-permute-start(f32[32,1,512]{2,1,0:T(1,128)S(1)} %get-tuple-element.150), channel_id=1, source_target_pairs={{0,2},{2,4},{4,6},{6,8},{8,10},{10,12},{12,14},{14,16},{16,18},{18... | collective-permute-start | bytes 196616 | tf_op jit(solution)/shard_map/while/body/ppermute | solution.py:14
  455.0 6.2 %collective-permute-start.1 = (f32[32,1,512]{2,1,0:T(1,128)S(1)}, f32[32,1,512]{2,1,0:T(1,128)S(1)}, u32[]{:S(2)}, u32[]{:S(2)}) collective-permute-start(f32[32,1,512]{2,1,0:T(1,128)S(1)} %get-tuple-element.150), channel_id=1, source_target_pairs={{0,2},{2,4},{4,6},{6,8},{8,10},{10,12},{12,14},{14,16},{16,18},{18... | collective-permute-start | bytes 196616 | tf_op jit(solution)/shard_map/while/body/ppermute | solution.py:14
  466.5 3.6 copy.14
  470.1 2.9 gather_fusion
  473.7 3.3 all-to-all-start
  477.2 3.8 all-to-all-done
  481.4 50.6 %all-reduce.2 = (f32[64,64]{1,0:T(8,128)S(1)}, f32[64,64]{1,0:T(8,128)S(1)}) all-reduce(f32[64,64]{1,0:T(8,128)S(1)} %fusion.32, f32[64,64]{1,0:T(8,128)S(1)} %fusion.31), channel_id=1, replica_groups=mesh['space'=16,'ens'=2] {'space','ens'}, use_global_device_ids=true, to_apply=%region_7.8 | all-reduce | flops 8192 | bytes 65536 | tf_op jit(solution)/shard_map/psum | solution.py:83
  532.1 5.8 %cholesky.17 = f32[64,64]{1,0:T(8,128)S(1)} custom-call(f32[64,64]{1,0:T(8,128)S(1)} %fusion.23), custom_call_target="Cholesky" | custom-call | tf_op jit(solution)/shard_map/jit(cholesky)/cholesky | solution.py:51
  539.3 4.9 custom-call.8
  544.9 4.3 copy.17
  549.3 2.8 convolution_subtract_fusion
  (303 shorter events, 232.6 us)
Async XLA Ops:
  7.2 537.7 %all-gather.2.cloned.1.call-start = ((), (), s32[]{:S(2)}) async-start(), calls=%async_computation.1 | async-start | bytes 3145728 | tf_op jit(solution)/shard_map/all_gather | solution.py:86
  47.8 7.4 %collective-permute-start = (f32[32,1,512]{2,1,0:T(1,128)S(1)}, f32[32,1,512]{2,1,0:T(1,128)S(1)}, u32[]{:S(2)}, u32[]{:S(2)}) collective-permute-start(f32[32,1,512]{2,1,0:T(1,128)S(1)} %get-tuple-element.149), channel_id=1, source_target_pairs={{2,0},{4,2},{6,4},{8,6},{10,8},{12,10},{14,12},{16,14},{18,16},{20... | collective-permute-start | bytes 196616 | tf_op jit(solution)/shard_map/while/body/ppermute | solution.py:17
  75.1 7.4 %collective-permute-start = (f32[32,1,512]{2,1,0:T(1,128)S(1)}, f32[32,1,512]{2,1,0:T(1,128)S(1)}, u32[]{:S(2)}, u32[]{:S(2)}) collective-permute-start(f32[32,1,512]{2,1,0:T(1,128)S(1)} %get-tuple-element.149), channel_id=1, source_target_pairs={{2,0},{4,2},{6,4},{8,6},{10,8},{12,10},{14,12},{16,14},{18,16},{20... | collective-permute-start | bytes 196616 | tf_op jit(solution)/shard_map/while/body/ppermute | solution.py:17
  89.0 7.4 %collective-permute-start = (f32[32,1,512]{2,1,0:T(1,128)S(1)}, f32[32,1,512]{2,1,0:T(1,128)S(1)}, u32[]{:S(2)}, u32[]{:S(2)}) collective-permute-start(f32[32,1,512]{2,1,0:T(1,128)S(1)} %get-tuple-element.149), channel_id=1, source_target_pairs={{2,0},{4,2},{6,4},{8,6},{10,8},{12,10},{14,12},{16,14},{18,16},{20... | collective-permute-start | bytes 196616 | tf_op jit(solution)/shard_map/while/body/ppermute | solution.py:17
  142.7 7.5 %collective-permute-start = (f32[32,1,512]{2,1,0:T(1,128)S(1)}, f32[32,1,512]{2,1,0:T(1,128)S(1)}, u32[]{:S(2)}, u32[]{:S(2)}) collective-permute-start(f32[32,1,512]{2,1,0:T(1,128)S(1)} %get-tuple-element.149), channel_id=1, source_target_pairs={{2,0},{4,2},{6,4},{8,6},{10,8},{12,10},{14,12},{16,14},{18,16},{20... | collective-permute-start | bytes 196616 | tf_op jit(solution)/shard_map/while/body/ppermute | solution.py:17
  144.0 7.1 %collective-permute-start.1 = (f32[32,1,512]{2,1,0:T(1,128)S(1)}, f32[32,1,512]{2,1,0:T(1,128)S(1)}, u32[]{:S(2)}, u32[]{:S(2)}) collective-permute-start(f32[32,1,512]{2,1,0:T(1,128)S(1)} %get-tuple-element.150), channel_id=1, source_target_pairs={{0,2},{2,4},{4,6},{6,8},{8,10},{10,12},{12,14},{14,16},{16,18},{18... | collective-permute-start | bytes 196616 | tf_op jit(solution)/shard_map/while/body/ppermute | solution.py:14
  156.9 7.5 %collective-permute-start = (f32[32,1,512]{2,1,0:T(1,128)S(1)}, f32[32,1,512]{2,1,0:T(1,128)S(1)}, u32[]{:S(2)}, u32[]{:S(2)}) collective-permute-start(f32[32,1,512]{2,1,0:T(1,128)S(1)} %get-tuple-element.149), channel_id=1, source_target_pairs={{2,0},{4,2},{6,4},{8,6},{10,8},{12,10},{14,12},{16,14},{18,16},{20... | collective-permute-start | bytes 196616 | tf_op jit(solution)/shard_map/while/body/ppermute | solution.py:17
  158.2 7.1 %collective-permute-start.1 = (f32[32,1,512]{2,1,0:T(1,128)S(1)}, f32[32,1,512]{2,1,0:T(1,128)S(1)}, u32[]{:S(2)}, u32[]{:S(2)}) collective-permute-start(f32[32,1,512]{2,1,0:T(1,128)S(1)} %get-tuple-element.150), channel_id=1, source_target_pairs={{0,2},{2,4},{4,6},{6,8},{8,10},{10,12},{12,14},{14,16},{16,18},{18... | collective-permute-start | bytes 196616 | tf_op jit(solution)/shard_map/while/body/ppermute | solution.py:14
  171.0 7.5 %collective-permute-start = (f32[32,1,512]{2,1,0:T(1,128)S(1)}, f32[32,1,512]{2,1,0:T(1,128)S(1)}, u32[]{:S(2)}, u32[]{:S(2)}) collective-permute-start(f32[32,1,512]{2,1,0:T(1,128)S(1)} %get-tuple-element.149), channel_id=1, source_target_pairs={{2,0},{4,2},{6,4},{8,6},{10,8},{12,10},{14,12},{16,14},{18,16},{20... | collective-permute-start | bytes 196616 | tf_op jit(solution)/shard_map/while/body/ppermute | solution.py:17
  172.3 7.1 %collective-permute-start.1 = (f32[32,1,512]{2,1,0:T(1,128)S(1)}, f32[32,1,512]{2,1,0:T(1,128)S(1)}, u32[]{:S(2)}, u32[]{:S(2)}) collective-permute-start(f32[32,1,512]{2,1,0:T(1,128)S(1)} %get-tuple-element.150), channel_id=1, source_target_pairs={{0,2},{2,4},{4,6},{6,8},{8,10},{10,12},{12,14},{14,16},{16,18},{18... | collective-permute-start | bytes 196616 | tf_op jit(solution)/shard_map/while/body/ppermute | solution.py:14
  185.1 7.5 %collective-permute-start = (f32[32,1,512]{2,1,0:T(1,128)S(1)}, f32[32,1,512]{2,1,0:T(1,128)S(1)}, u32[]{:S(2)}, u32[]{:S(2)}) collective-permute-start(f32[32,1,512]{2,1,0:T(1,128)S(1)} %get-tuple-element.149), channel_id=1, source_target_pairs={{2,0},{4,2},{6,4},{8,6},{10,8},{12,10},{14,12},{16,14},{18,16},{20... | collective-permute-start | bytes 196616 | tf_op jit(solution)/shard_map/while/body/ppermute | solution.py:17
  186.4 7.1 %collective-permute-start.1 = (f32[32,1,512]{2,1,0:T(1,128)S(1)}, f32[32,1,512]{2,1,0:T(1,128)S(1)}, u32[]{:S(2)}, u32[]{:S(2)}) collective-permute-start(f32[32,1,512]{2,1,0:T(1,128)S(1)} %get-tuple-element.150), channel_id=1, source_target_pairs={{0,2},{2,4},{4,6},{6,8},{8,10},{10,12},{12,14},{14,16},{16,18},{18... | collective-permute-start | bytes 196616 | tf_op jit(solution)/shard_map/while/body/ppermute | solution.py:14
  199.3 7.5 %collective-permute-start = (f32[32,1,512]{2,1,0:T(1,128)S(1)}, f32[32,1,512]{2,1,0:T(1,128)S(1)}, u32[]{:S(2)}, u32[]{:S(2)}) collective-permute-start(f32[32,1,512]{2,1,0:T(1,128)S(1)} %get-tuple-element.149), channel_id=1, source_target_pairs={{2,0},{4,2},{6,4},{8,6},{10,8},{12,10},{14,12},{16,14},{18,16},{20... | collective-permute-start | bytes 196616 | tf_op jit(solution)/shard_map/while/body/ppermute | solution.py:17
  200.6 7.1 %collective-permute-start.1 = (f32[32,1,512]{2,1,0:T(1,128)S(1)}, f32[32,1,512]{2,1,0:T(1,128)S(1)}, u32[]{:S(2)}, u32[]{:S(2)}) collective-permute-start(f32[32,1,512]{2,1,0:T(1,128)S(1)} %get-tuple-element.150), channel_id=1, source_target_pairs={{0,2},{2,4},{4,6},{6,8},{8,10},{10,12},{12,14},{14,16},{16,18},{18... | collective-permute-start | bytes 196616 | tf_op jit(solution)/shard_map/while/body/ppermute | solution.py:14
  213.4 7.5 %collective-permute-start = (f32[32,1,512]{2,1,0:T(1,128)S(1)}, f32[32,1,512]{2,1,0:T(1,128)S(1)}, u32[]{:S(2)}, u32[]{:S(2)}) collective-permute-start(f32[32,1,512]{2,1,0:T(1,128)S(1)} %get-tuple-element.149), channel_id=1, source_target_pairs={{2,0},{4,2},{6,4},{8,6},{10,8},{12,10},{14,12},{16,14},{18,16},{20... | collective-permute-start | bytes 196616 | tf_op jit(solution)/shard_map/while/body/ppermute | solution.py:17
  214.7 7.1 %collective-permute-start.1 = (f32[32,1,512]{2,1,0:T(1,128)S(1)}, f32[32,1,512]{2,1,0:T(1,128)S(1)}, u32[]{:S(2)}, u32[]{:S(2)}) collective-permute-start(f32[32,1,512]{2,1,0:T(1,128)S(1)} %get-tuple-element.150), channel_id=1, source_target_pairs={{0,2},{2,4},{4,6},{6,8},{8,10},{10,12},{12,14},{14,16},{16,18},{18... | collective-permute-start | bytes 196616 | tf_op jit(solution)/shard_map/while/body/ppermute | solution.py:14
  227.5 7.5 %collective-permute-start = (f32[32,1,512]{2,1,0:T(1,128)S(1)}, f32[32,1,512]{2,1,0:T(1,128)S(1)}, u32[]{:S(2)}, u32[]{:S(2)}) collective-permute-start(f32[32,1,512]{2,1,0:T(1,128)S(1)} %get-tuple-element.149), channel_id=1, source_target_pairs={{2,0},{4,2},{6,4},{8,6},{10,8},{12,10},{14,12},{16,14},{18,16},{20... | collective-permute-start | bytes 196616 | tf_op jit(solution)/shard_map/while/body/ppermute | solution.py:17
  228.8 7.1 %collective-permute-start.1 = (f32[32,1,512]{2,1,0:T(1,128)S(1)}, f32[32,1,512]{2,1,0:T(1,128)S(1)}, u32[]{:S(2)}, u32[]{:S(2)}) collective-permute-start(f32[32,1,512]{2,1,0:T(1,128)S(1)} %get-tuple-element.150), channel_id=1, source_target_pairs={{0,2},{2,4},{4,6},{6,8},{8,10},{10,12},{12,14},{14,16},{16,18},{18... | collective-permute-start | bytes 196616 | tf_op jit(solution)/shard_map/while/body/ppermute | solution.py:14
  241.7 7.5 %collective-permute-start = (f32[32,1,512]{2,1,0:T(1,128)S(1)}, f32[32,1,512]{2,1,0:T(1,128)S(1)}, u32[]{:S(2)}, u32[]{:S(2)}) collective-permute-start(f32[32,1,512]{2,1,0:T(1,128)S(1)} %get-tuple-element.149), channel_id=1, source_target_pairs={{2,0},{4,2},{6,4},{8,6},{10,8},{12,10},{14,12},{16,14},{18,16},{20... | collective-permute-start | bytes 196616 | tf_op jit(solution)/shard_map/while/body/ppermute | solution.py:17
  243.0 7.1 %collective-permute-start.1 = (f32[32,1,512]{2,1,0:T(1,128)S(1)}, f32[32,1,512]{2,1,0:T(1,128)S(1)}, u32[]{:S(2)}, u32[]{:S(2)}) collective-permute-start(f32[32,1,512]{2,1,0:T(1,128)S(1)} %get-tuple-element.150), channel_id=1, source_target_pairs={{0,2},{2,4},{4,6},{6,8},{8,10},{10,12},{12,14},{14,16},{16,18},{18... | collective-permute-start | bytes 196616 | tf_op jit(solution)/shard_map/while/body/ppermute | solution.py:14
  255.8 7.5 %collective-permute-start = (f32[32,1,512]{2,1,0:T(1,128)S(1)}, f32[32,1,512]{2,1,0:T(1,128)S(1)}, u32[]{:S(2)}, u32[]{:S(2)}) collective-permute-start(f32[32,1,512]{2,1,0:T(1,128)S(1)} %get-tuple-element.149), channel_id=1, source_target_pairs={{2,0},{4,2},{6,4},{8,6},{10,8},{12,10},{14,12},{16,14},{18,16},{20... | collective-permute-start | bytes 196616 | tf_op jit(solution)/shard_map/while/body/ppermute | solution.py:17
  257.1 7.1 %collective-permute-start.1 = (f32[32,1,512]{2,1,0:T(1,128)S(1)}, f32[32,1,512]{2,1,0:T(1,128)S(1)}, u32[]{:S(2)}, u32[]{:S(2)}) collective-permute-start(f32[32,1,512]{2,1,0:T(1,128)S(1)} %get-tuple-element.150), channel_id=1, source_target_pairs={{0,2},{2,4},{4,6},{6,8},{8,10},{10,12},{12,14},{14,16},{16,18},{18... | collective-permute-start | bytes 196616 | tf_op jit(solution)/shard_map/while/body/ppermute | solution.py:14
  269.9 7.5 %collective-permute-start = (f32[32,1,512]{2,1,0:T(1,128)S(1)}, f32[32,1,512]{2,1,0:T(1,128)S(1)}, u32[]{:S(2)}, u32[]{:S(2)}) collective-permute-start(f32[32,1,512]{2,1,0:T(1,128)S(1)} %get-tuple-element.149), channel_id=1, source_target_pairs={{2,0},{4,2},{6,4},{8,6},{10,8},{12,10},{14,12},{16,14},{18,16},{20... | collective-permute-start | bytes 196616 | tf_op jit(solution)/shard_map/while/body/ppermute | solution.py:17
  271.2 7.1 %collective-permute-start.1 = (f32[32,1,512]{2,1,0:T(1,128)S(1)}, f32[32,1,512]{2,1,0:T(1,128)S(1)}, u32[]{:S(2)}, u32[]{:S(2)}) collective-permute-start(f32[32,1,512]{2,1,0:T(1,128)S(1)} %get-tuple-element.150), channel_id=1, source_target_pairs={{0,2},{2,4},{4,6},{6,8},{8,10},{10,12},{12,14},{14,16},{16,18},{18... | collective-permute-start | bytes 196616 | tf_op jit(solution)/shard_map/while/body/ppermute | solution.py:14
  284.1 7.5 %collective-permute-start = (f32[32,1,512]{2,1,0:T(1,128)S(1)}, f32[32,1,512]{2,1,0:T(1,128)S(1)}, u32[]{:S(2)}, u32[]{:S(2)}) collective-permute-start(f32[32,1,512]{2,1,0:T(1,128)S(1)} %get-tuple-element.149), channel_id=1, source_target_pairs={{2,0},{4,2},{6,4},{8,6},{10,8},{12,10},{14,12},{16,14},{18,16},{20... | collective-permute-start | bytes 196616 | tf_op jit(solution)/shard_map/while/body/ppermute | solution.py:17
  285.4 7.1 %collective-permute-start.1 = (f32[32,1,512]{2,1,0:T(1,128)S(1)}, f32[32,1,512]{2,1,0:T(1,128)S(1)}, u32[]{:S(2)}, u32[]{:S(2)}) collective-permute-start(f32[32,1,512]{2,1,0:T(1,128)S(1)} %get-tuple-element.150), channel_id=1, source_target_pairs={{0,2},{2,4},{4,6},{6,8},{8,10},{10,12},{12,14},{14,16},{16,18},{18... | collective-permute-start | bytes 196616 | tf_op jit(solution)/shard_map/while/body/ppermute | solution.py:14
  298.2 7.5 %collective-permute-start = (f32[32,1,512]{2,1,0:T(1,128)S(1)}, f32[32,1,512]{2,1,0:T(1,128)S(1)}, u32[]{:S(2)}, u32[]{:S(2)}) collective-permute-start(f32[32,1,512]{2,1,0:T(1,128)S(1)} %get-tuple-element.149), channel_id=1, source_target_pairs={{2,0},{4,2},{6,4},{8,6},{10,8},{12,10},{14,12},{16,14},{18,16},{20... | collective-permute-start | bytes 196616 | tf_op jit(solution)/shard_map/while/body/ppermute | solution.py:17
  299.5 7.1 %collective-permute-start.1 = (f32[32,1,512]{2,1,0:T(1,128)S(1)}, f32[32,1,512]{2,1,0:T(1,128)S(1)}, u32[]{:S(2)}, u32[]{:S(2)}) collective-permute-start(f32[32,1,512]{2,1,0:T(1,128)S(1)} %get-tuple-element.150), channel_id=1, source_target_pairs={{0,2},{2,4},{4,6},{6,8},{8,10},{10,12},{12,14},{14,16},{16,18},{18... | collective-permute-start | bytes 196616 | tf_op jit(solution)/shard_map/while/body/ppermute | solution.py:14
  312.3 7.5 %collective-permute-start = (f32[32,1,512]{2,1,0:T(1,128)S(1)}, f32[32,1,512]{2,1,0:T(1,128)S(1)}, u32[]{:S(2)}, u32[]{:S(2)}) collective-permute-start(f32[32,1,512]{2,1,0:T(1,128)S(1)} %get-tuple-element.149), channel_id=1, source_target_pairs={{2,0},{4,2},{6,4},{8,6},{10,8},{12,10},{14,12},{16,14},{18,16},{20... | collective-permute-start | bytes 196616 | tf_op jit(solution)/shard_map/while/body/ppermute | solution.py:17
  313.6 7.1 %collective-permute-start.1 = (f32[32,1,512]{2,1,0:T(1,128)S(1)}, f32[32,1,512]{2,1,0:T(1,128)S(1)}, u32[]{:S(2)}, u32[]{:S(2)}) collective-permute-start(f32[32,1,512]{2,1,0:T(1,128)S(1)} %get-tuple-element.150), channel_id=1, source_target_pairs={{0,2},{2,4},{4,6},{6,8},{8,10},{10,12},{12,14},{14,16},{16,18},{18... | collective-permute-start | bytes 196616 | tf_op jit(solution)/shard_map/while/body/ppermute | solution.py:14
  326.5 7.5 %collective-permute-start = (f32[32,1,512]{2,1,0:T(1,128)S(1)}, f32[32,1,512]{2,1,0:T(1,128)S(1)}, u32[]{:S(2)}, u32[]{:S(2)}) collective-permute-start(f32[32,1,512]{2,1,0:T(1,128)S(1)} %get-tuple-element.149), channel_id=1, source_target_pairs={{2,0},{4,2},{6,4},{8,6},{10,8},{12,10},{14,12},{16,14},{18,16},{20... | collective-permute-start | bytes 196616 | tf_op jit(solution)/shard_map/while/body/ppermute | solution.py:17
  327.8 7.1 %collective-permute-start.1 = (f32[32,1,512]{2,1,0:T(1,128)S(1)}, f32[32,1,512]{2,1,0:T(1,128)S(1)}, u32[]{:S(2)}, u32[]{:S(2)}) collective-permute-start(f32[32,1,512]{2,1,0:T(1,128)S(1)} %get-tuple-element.150), channel_id=1, source_target_pairs={{0,2},{2,4},{4,6},{6,8},{8,10},{10,12},{12,14},{14,16},{16,18},{18... | collective-permute-start | bytes 196616 | tf_op jit(solution)/shard_map/while/body/ppermute | solution.py:14
  340.6 7.5 %collective-permute-start = (f32[32,1,512]{2,1,0:T(1,128)S(1)}, f32[32,1,512]{2,1,0:T(1,128)S(1)}, u32[]{:S(2)}, u32[]{:S(2)}) collective-permute-start(f32[32,1,512]{2,1,0:T(1,128)S(1)} %get-tuple-element.149), channel_id=1, source_target_pairs={{2,0},{4,2},{6,4},{8,6},{10,8},{12,10},{14,12},{16,14},{18,16},{20... | collective-permute-start | bytes 196616 | tf_op jit(solution)/shard_map/while/body/ppermute | solution.py:17
  341.9 7.1 %collective-permute-start.1 = (f32[32,1,512]{2,1,0:T(1,128)S(1)}, f32[32,1,512]{2,1,0:T(1,128)S(1)}, u32[]{:S(2)}, u32[]{:S(2)}) collective-permute-start(f32[32,1,512]{2,1,0:T(1,128)S(1)} %get-tuple-element.150), channel_id=1, source_target_pairs={{0,2},{2,4},{4,6},{6,8},{8,10},{10,12},{12,14},{14,16},{16,18},{18... | collective-permute-start | bytes 196616 | tf_op jit(solution)/shard_map/while/body/ppermute | solution.py:14
  354.8 7.5 %collective-permute-start = (f32[32,1,512]{2,1,0:T(1,128)S(1)}, f32[32,1,512]{2,1,0:T(1,128)S(1)}, u32[]{:S(2)}, u32[]{:S(2)}) collective-permute-start(f32[32,1,512]{2,1,0:T(1,128)S(1)} %get-tuple-element.149), channel_id=1, source_target_pairs={{2,0},{4,2},{6,4},{8,6},{10,8},{12,10},{14,12},{16,14},{18,16},{20... | collective-permute-start | bytes 196616 | tf_op jit(solution)/shard_map/while/body/ppermute | solution.py:17
  356.1 7.1 %collective-permute-start.1 = (f32[32,1,512]{2,1,0:T(1,128)S(1)}, f32[32,1,512]{2,1,0:T(1,128)S(1)}, u32[]{:S(2)}, u32[]{:S(2)}) collective-permute-start(f32[32,1,512]{2,1,0:T(1,128)S(1)} %get-tuple-element.150), channel_id=1, source_target_pairs={{0,2},{2,4},{4,6},{6,8},{8,10},{10,12},{12,14},{14,16},{16,18},{18... | collective-permute-start | bytes 196616 | tf_op jit(solution)/shard_map/while/body/ppermute | solution.py:14
  368.9 7.5 %collective-permute-start = (f32[32,1,512]{2,1,0:T(1,128)S(1)}, f32[32,1,512]{2,1,0:T(1,128)S(1)}, u32[]{:S(2)}, u32[]{:S(2)}) collective-permute-start(f32[32,1,512]{2,1,0:T(1,128)S(1)} %get-tuple-element.149), channel_id=1, source_target_pairs={{2,0},{4,2},{6,4},{8,6},{10,8},{12,10},{14,12},{16,14},{18,16},{20... | collective-permute-start | bytes 196616 | tf_op jit(solution)/shard_map/while/body/ppermute | solution.py:17
  370.2 7.1 %collective-permute-start.1 = (f32[32,1,512]{2,1,0:T(1,128)S(1)}, f32[32,1,512]{2,1,0:T(1,128)S(1)}, u32[]{:S(2)}, u32[]{:S(2)}) collective-permute-start(f32[32,1,512]{2,1,0:T(1,128)S(1)} %get-tuple-element.150), channel_id=1, source_target_pairs={{0,2},{2,4},{4,6},{6,8},{8,10},{10,12},{12,14},{14,16},{16,18},{18... | collective-permute-start | bytes 196616 | tf_op jit(solution)/shard_map/while/body/ppermute | solution.py:14
  383.0 7.5 %collective-permute-start = (f32[32,1,512]{2,1,0:T(1,128)S(1)}, f32[32,1,512]{2,1,0:T(1,128)S(1)}, u32[]{:S(2)}, u32[]{:S(2)}) collective-permute-start(f32[32,1,512]{2,1,0:T(1,128)S(1)} %get-tuple-element.149), channel_id=1, source_target_pairs={{2,0},{4,2},{6,4},{8,6},{10,8},{12,10},{14,12},{16,14},{18,16},{20... | collective-permute-start | bytes 196616 | tf_op jit(solution)/shard_map/while/body/ppermute | solution.py:17
  384.3 7.1 %collective-permute-start.1 = (f32[32,1,512]{2,1,0:T(1,128)S(1)}, f32[32,1,512]{2,1,0:T(1,128)S(1)}, u32[]{:S(2)}, u32[]{:S(2)}) collective-permute-start(f32[32,1,512]{2,1,0:T(1,128)S(1)} %get-tuple-element.150), channel_id=1, source_target_pairs={{0,2},{2,4},{4,6},{6,8},{8,10},{10,12},{12,14},{14,16},{16,18},{18... | collective-permute-start | bytes 196616 | tf_op jit(solution)/shard_map/while/body/ppermute | solution.py:14
  397.2 7.5 %collective-permute-start = (f32[32,1,512]{2,1,0:T(1,128)S(1)}, f32[32,1,512]{2,1,0:T(1,128)S(1)}, u32[]{:S(2)}, u32[]{:S(2)}) collective-permute-start(f32[32,1,512]{2,1,0:T(1,128)S(1)} %get-tuple-element.149), channel_id=1, source_target_pairs={{2,0},{4,2},{6,4},{8,6},{10,8},{12,10},{14,12},{16,14},{18,16},{20... | collective-permute-start | bytes 196616 | tf_op jit(solution)/shard_map/while/body/ppermute | solution.py:17
  411.3 7.5 %collective-permute-start = (f32[32,1,512]{2,1,0:T(1,128)S(1)}, f32[32,1,512]{2,1,0:T(1,128)S(1)}, u32[]{:S(2)}, u32[]{:S(2)}) collective-permute-start(f32[32,1,512]{2,1,0:T(1,128)S(1)} %get-tuple-element.149), channel_id=1, source_target_pairs={{2,0},{4,2},{6,4},{8,6},{10,8},{12,10},{14,12},{16,14},{18,16},{20... | collective-permute-start | bytes 196616 | tf_op jit(solution)/shard_map/while/body/ppermute | solution.py:17
  412.6 7.1 %collective-permute-start.1 = (f32[32,1,512]{2,1,0:T(1,128)S(1)}, f32[32,1,512]{2,1,0:T(1,128)S(1)}, u32[]{:S(2)}, u32[]{:S(2)}) collective-permute-start(f32[32,1,512]{2,1,0:T(1,128)S(1)} %get-tuple-element.150), channel_id=1, source_target_pairs={{0,2},{2,4},{4,6},{6,8},{8,10},{10,12},{12,14},{14,16},{16,18},{18... | collective-permute-start | bytes 196616 | tf_op jit(solution)/shard_map/while/body/ppermute | solution.py:14
  425.4 7.5 %collective-permute-start = (f32[32,1,512]{2,1,0:T(1,128)S(1)}, f32[32,1,512]{2,1,0:T(1,128)S(1)}, u32[]{:S(2)}, u32[]{:S(2)}) collective-permute-start(f32[32,1,512]{2,1,0:T(1,128)S(1)} %get-tuple-element.149), channel_id=1, source_target_pairs={{2,0},{4,2},{6,4},{8,6},{10,8},{12,10},{14,12},{16,14},{18,16},{20... | collective-permute-start | bytes 196616 | tf_op jit(solution)/shard_map/while/body/ppermute | solution.py:17
  439.6 7.5 %collective-permute-start = (f32[32,1,512]{2,1,0:T(1,128)S(1)}, f32[32,1,512]{2,1,0:T(1,128)S(1)}, u32[]{:S(2)}, u32[]{:S(2)}) collective-permute-start(f32[32,1,512]{2,1,0:T(1,128)S(1)} %get-tuple-element.149), channel_id=1, source_target_pairs={{2,0},{4,2},{6,4},{8,6},{10,8},{12,10},{14,12},{16,14},{18,16},{20... | collective-permute-start | bytes 196616 | tf_op jit(solution)/shard_map/while/body/ppermute | solution.py:17
  440.9 7.1 %collective-permute-start.1 = (f32[32,1,512]{2,1,0:T(1,128)S(1)}, f32[32,1,512]{2,1,0:T(1,128)S(1)}, u32[]{:S(2)}, u32[]{:S(2)}) collective-permute-start(f32[32,1,512]{2,1,0:T(1,128)S(1)} %get-tuple-element.150), channel_id=1, source_target_pairs={{0,2},{2,4},{4,6},{6,8},{8,10},{10,12},{12,14},{14,16},{16,18},{18... | collective-permute-start | bytes 196616 | tf_op jit(solution)/shard_map/while/body/ppermute | solution.py:14
  453.7 7.5 %collective-permute-start = (f32[32,1,512]{2,1,0:T(1,128)S(1)}, f32[32,1,512]{2,1,0:T(1,128)S(1)}, u32[]{:S(2)}, u32[]{:S(2)}) collective-permute-start(f32[32,1,512]{2,1,0:T(1,128)S(1)} %get-tuple-element.149), channel_id=1, source_target_pairs={{2,0},{4,2},{6,4},{8,6},{10,8},{12,10},{14,12},{16,14},{18,16},{20... | collective-permute-start | bytes 196616 | tf_op jit(solution)/shard_map/while/body/ppermute | solution.py:17
  473.7 7.2 %all-to-all-start = ((f32[32,2,128]{2,0,1:T(8,128)}), f32[32,2,128]{2,0,1:T(8,128)S(1)}, u32[]{:S(2)}, u32[]{:S(2)}) async-start(f32[32,2,128]{2,0,1:T(8,128)} %broadcast_select_fusion), calls=%async_computation | async-start | bytes 65536 | tf_op jit(solution)/shard_map/all_to_all | solution.py:78
  (28 other events, 184.5 us)
Sparse Core Ops, SparseCore 0:
  9.5 35.8 all-gather.1
where the time goes:
time: 566 us; the launch traced here: 561 us
  starting transfers between devices  242 us (43%)
  other arithmetic  136 us (24%)
  local copies, waits for them, and re-layouts  57.3 us (10%)
  blocking collectives  50.6 us (9%)
  waiting for transfers between devices  35.1 us (6%)
  loops' own time  21.8 us (4%)
  between operations  14.3 us (3%)
    ppermute x33, starting transfers between devices, padded_2(): lax.ppermute(lax.slice_in_dim(block, block.shape[dim] - width, None, axis...  196 us
    select_n x32, other arithmetic, advance(): return jnp.where((step_index < own_counts)[:, None, None], moved, thickness)  87.3 us
    psum x1, blocking collectives, shards(): gram, cross = lax.psum((gram, cross), ('space', 'ens'))  50.6 us
    ppermute x33, starting transfers between devices, padded_2(): lax.ppermute(lax.slice_in_dim(block, 0, width, axis=dim), axis, backward)  42.6 us
    while x32, local copies, waits for them, and re-layouts  39.3 us
    div x32, other arithmetic, stencil(): diffusivity = slip_padded * padded * padded / (1.0 + padded * padded)  32.8 us
    ppermute x33, waiting for transfers between devices, padded_2(): lax.ppermute(lax.slice_in_dim(block, block.shape[dim] - width, None, axis...  27.4 us
    another operation x1, loops' own time, shards(): thickness = lax.fori_loop(0, longest, advance, initial)  21.8 us
  transfers between devices with their start and end apart: 68, of which 34 were waited for; matrix products, arithmetic and copies ran while one was open for 34% of the time, Pallas kernels for 0%

commit v1 on v0

v1 whole, which is shorter than its diff:
```python
import functools
import jax
import jax.numpy as jnp
from jax import lax
from jax.experimental import pallas as pl
from jax.experimental.pallas import tpu as pltpu
from jax.sharding import PartitionSpec as P

time_step = 0.11
steps = 32
halo = 4
sub = 8
lane = 128
MESH = pl.DeviceIdType.MESH


def reciprocal(x):
    r = pl.reciprocal(x, approx=True)
    return r * (2.0 - x * r)


def substep(h_ref, slip_ref, bal_ref, group, first, last, masks, rows):
    pieces = h_ref.shape[-1] // lane
    lanes = lax.broadcasted_iota(jnp.int32, (sub, lane), 1)
    at_end = lanes == lane - 1
    at_start = lanes == 0
    cols = [pl.ds(p * lane, lane) for p in range(pieces)]
    zero = jnp.zeros((sub, lane), jnp.float32)
    prev = None
    for row in range(first, last):
        h = [h_ref[group, row, :, c] for c in cols]
        d = []
        for p, c in enumerate(cols):
            square = h[p] * h[p]
            d.append(slip_ref[group, row, :, c] * square * reciprocal(1.0 + square))
        if prev is not None:
            prev_h, prev_d, prev_down = prev
            down = [(d[p] + prev_d[p]) * (h[p] - prev_h[p]) for p in range(pieces)]
            if prev_down is not None:
                out = row - 1
                mask = masks[0] if out < halo else masks[1] if out < halo + rows else masks[2]
                h_rot = [pltpu.roll(prev_h[p], lane - 1, 1) for p in range(pieces)] + [zero]
                d_rot = [pltpu.roll(prev_d[p], lane - 1, 1) for p in range(pieces)] + [zero]
                flux = []
                for p in range(pieces):
                    h_right = jnp.where(at_end, h_rot[p + 1], h_rot[p])
                    d_right = jnp.where(at_end, d_rot[p + 1], d_rot[p])
                    flux.append((d_right + prev_d[p]) * (h_right - prev_h[p]))
                f_rot = [pltpu.roll(flux[p], 1, 1) for p in range(pieces)]
                for p, c in enumerate(cols):
                    edge = prev_d[0] * prev_h[0] if p == 0 else f_rot[p - 1]
                    f_left = jnp.where(at_start, edge, f_rot[p])
                    change = (down[p] - prev_down[p]) + (flux[p] - f_left)
                    moved = (prev_h[p] + bal_ref[out, :, c]) + change
                    h_ref[group, out, :, c] = jnp.where(mask, moved, prev_h[p])
        else:
            down = None
        prev = (h, d, down)


def advance_kernel(
    spaces, enss, params_ref, params_any, bb_ref, count_ref, out_ref, gathered,
    h_ref, slip_ref, bal_ref, land_ref, bb_land,
    send_sem, recv_sem, slip_send, slip_recv, bb_send, bb_recv, ens_send, ens_recv, own_sem,
):
    members, rows, width = params_ref.shape
    groups = members // sub
    total = rows + 2 * halo
    blocks = steps // halo
    me = lax.axis_index("space")
    ens = lax.axis_index("ens")
    has_up = me > 0
    has_down = me < spaces - 1
    up = jnp.maximum(me - 1, 0)
    down = jnp.minimum(me + 1, spaces - 1)
    others = [lax.rem(ens + step, enss) for step in range(1, enss)]

    barrier = pltpu.get_barrier_semaphore()

    @pl.when(has_up)
    def _():
        pl.semaphore_signal(barrier, inc=1, device_id={"space": up}, device_id_type=MESH)

    @pl.when(has_down)
    def _():
        pl.semaphore_signal(barrier, inc=1, device_id={"space": down}, device_id_type=MESH)

    for other in others:
        pl.semaphore_signal(barrier, inc=1, device_id={"ens": other}, device_id_type=MESH)
    neighbours = has_up.astype(jnp.int32) + has_down.astype(jnp.int32) + (enss - 1)
    pl.semaphore_wait(barrier, neighbours)

    sides = (
        (has_up, up, pl.ds(halo, halo), pl.ds(halo + rows, halo), 1),
        (has_down, down, pl.ds(rows, halo), pl.ds(0, halo), 0),
    )
    own_rows = (pl.ds(0, halo), pl.ds(rows - halo, halo))

    def bb_copy(side):
        _, target, _, _, there = sides[side]
        return pltpu.make_async_remote_copy(
            bb_ref.at[own_rows[side]], bb_land.at[there], bb_send.at[side], bb_recv.at[there],
            device_id={"space": target}, device_id_type=MESH,
        )

    def slip_copy(group, side):
        _, target, source, dest, there = sides[side]
        return pltpu.make_async_remote_copy(
            slip_ref.at[group, source], slip_ref.at[group, dest],
            slip_send.at[group, side], slip_recv.at[group, there],
            device_id={"space": target}, device_id_type=MESH,
        )

    def slip_arrival(group, side):
        _, target, _, _, _ = sides[side]
        here = pl.ds(0, halo) if side == 0 else pl.ds(halo + rows, halo)
        return pltpu.make_async_remote_copy(
            slip_ref.at[group, here], slip_ref.at[group, here],
            slip_send.at[group, side], slip_recv.at[group, side],
            device_id={"space": target}, device_id_type=MESH,
        )

    def h_copy(group, side, slot):
        _, target, source, _, there = sides[side]
        return pltpu.make_async_remote_copy(
            h_ref.at[group, source], land_ref.at[group, slot, there],
            send_sem.at[group, side], recv_sem.at[group, slot, there],
            device_id={"space": target}, device_id_type=MESH,
        )

    def h_arrival(group, side, slot):
        _, target, source, _, _ = sides[side]
        return pltpu.make_async_remote_copy(
            h_ref.at[group, source], land_ref.at[group, slot, side],
            send_sem.at[group, side], recv_sem.at[group, slot, side],
            device_id={"space": target}, device_id_type=MESH,
        )

    def bb_arrival(side):
        _, target, _, _, _ = sides[side]
        return pltpu.make_async_remote_copy(
            bb_ref.at[own_rows[side]], bb_land.at[side], bb_send.at[side], bb_recv.at[side],
            device_id={"space": target}, device_id_type=MESH,
        )

    for side in range(2):
        @pl.when(sides[side][0])
        def _(side=side):
            bb_copy(side).start()

    @pl.loop(0, groups)
    def _(group):
        block = params_ref[pl.ds(group * sub, sub)]
        turned = jnp.swapaxes(jnp.exp(block) * (0.5 * time_step), 0, 1)
        slip_ref[group, pl.ds(halo, rows)] = turned
        for side in range(2):
            @pl.when(sides[side][0])
            def _(side=side):
                slip_copy(group, side).start()

    def ens_copy(step):
        return pltpu.make_async_remote_copy(
            params_any, gathered.at[ens], ens_send.at[step], ens_recv.at[step],
            device_id={"ens": others[step]}, device_id_type=MESH,
        )

    for step in range(enss - 1):
        ens_copy(step).start()
    own_copy = pltpu.make_async_copy(params_ref, gathered.at[ens], own_sem)
    own_copy.start()

    def wide(row):
        return jnp.broadcast_to(row, (sub, width))

    @pl.loop(0, rows)
    def _(row):
        base = wide(bb_ref[row, 0:1, :])
        for group in range(groups):
            h_ref[group, row + halo] = base
        bal_ref[row + halo] = wide(bb_ref[row, 1:2, :]) * time_step

    for side in range(2):
        begin = 0 if side == 0 else halo + rows

        @pl.when(sides[side][0])
        def _(side=side, begin=begin):
            bb_arrival(side).wait_recv()
            for row in range(halo):
                base = wide(bb_land[side, row, 0:1, :])
                for group in range(groups):
                    h_ref[group, begin + row] = base
                bal_ref[begin + row] = wide(bb_land[side, row, 1:2, :]) * time_step

        @pl.when(jnp.logical_not(sides[side][0]))
        def _(side=side, begin=begin):
            zero = jnp.zeros((sub, width), jnp.float32)
            for row in range(halo):
                for group in range(groups):
                    h_ref[group, begin + row] = zero
                    slip_ref[group, begin + row] = zero
                bal_ref[begin + row] = zero

    @pl.loop(0, blocks)
    def _(block):
        slot = lax.rem(block, 2)

        @pl.loop(0, groups)
        def _(group):
            for side in range(2):
                begin = 0 if side == 0 else halo + rows

                @pl.when(jnp.logical_and(sides[side][0], block == 0))
                def _(side=side):
                    slip_arrival(group, side).wait_recv()

                @pl.when(jnp.logical_and(sides[side][0], block > 0))
                def _(side=side, begin=begin):
                    h_copy(group, side, slot).wait_send()
                    h_arrival(group, side, slot).wait_recv()
                    h_ref[group, pl.ds(begin, halo)] = land_ref[group, slot, side]

            count = count_ref[group]
            counts = (
                count * has_up.astype(jnp.int32), count, count * has_down.astype(jnp.int32)
            )
            for step in range(halo):
                now = block * halo + step
                masks = [now < value for value in counts]
                substep(h_ref, slip_ref, bal_ref, group, step, total - step, masks, rows)

            for side in range(2):
                @pl.when(jnp.logical_and(sides[side][0], block < blocks - 1))
                def _(side=side):
                    h_copy(group, side, 1 - slot).start()

    for group in range(groups):
        out_ref[pl.ds(group * sub, sub)] = jnp.swapaxes(h_ref[group, pl.ds(halo, rows)], 0, 1)

    own_copy.wait()
    for step in range(enss - 1):
        ens_copy(step).wait()
    for side in range(2):
        @pl.when(sides[side][0])
        def _(side=side):
            bb_copy(side).wait_send()
            for group in range(groups):
                slip_copy(group, side).wait_send()


def advance(params, bb, counts, spaces, enss):
    members, rows, width = params.shape
    groups = members // sub
    total = rows + 2 * halo
    dma = pltpu.SemaphoreType.DMA
    vmem = pl.BlockSpec(memory_space=pltpu.VMEM)
    hbm = pl.BlockSpec(memory_space=pl.ANY)
    return pl.pallas_call(
        functools.partial(advance_kernel, spaces, enss),
        out_shape=(
            jax.ShapeDtypeStruct(params.shape, jnp.float32),
            jax.ShapeDtypeStruct((enss, members, rows, width), jnp.float32),
        ),
        in_specs=[vmem, hbm, vmem, vmem],
        out_specs=(vmem, hbm),
        scratch_shapes=[
            pltpu.VMEM((groups, total, sub, width), jnp.float32),
            pltpu.VMEM((groups, total, sub, width), jnp.float32),
            pltpu.VMEM((total, sub, width), jnp.float32),
            pltpu.VMEM((groups, 2, 2, halo, sub, width), jnp.float32),
            pltpu.VMEM((2, halo, 2, width), jnp.float32),
            dma((groups, 2)),
            dma((groups, 2, 2)),
            dma((groups, 2)),
            dma((groups, 2)),
            dma((2,)),
            dma((2,)),
            dma((max(enss - 1, 1),)),
            dma((max(enss - 1, 1),)),
            dma(()),
        ],
        compiler_params=pltpu.CompilerParams(
            collective_id=0, has_side_effects=True, vmem_limit_bytes=40 * 1024 * 1024
        ),
        name="advance",
    )(params, params, bb, counts)


def ensemble_terms(predicted, observed, noise_var):
    members = predicted.shape[0]
    scaling = lax.rsqrt(noise_var)
    average = jnp.mean(predicted, axis=0)
    anomalies = (predicted - average) * scaling / jnp.sqrt(jnp.float32(members - 1))
    mismatch = (observed - predicted) * scaling
    gram = jnp.dot(anomalies, anomalies.T, precision=lax.Precision.HIGHEST)
    cross = jnp.dot(anomalies, mismatch.T, precision=lax.Precision.HIGHEST)
    return (gram, cross)


def solve_weights(gram, cross):
    members = gram.shape[0]
    factor = jnp.linalg.cholesky(gram + jnp.eye(members, dtype=gram.dtype))
    inner = lax.linalg.triangular_solve(factor, cross, left_side=True, lower=True)
    result = lax.linalg.triangular_solve(
        factor, inner, left_side=True, lower=True, transpose_a=True
    )
    return result / jnp.sqrt(jnp.float32(members - 1))


def shards(params, base_thickness, balance, step_count, obs_index, observed, noise_var):
    members_dev = params.shape[0]
    ens_index = lax.axis_index("ens")
    enss = lax.axis_size("ens")
    members = members_dev * enss
    own_counts = lax.dynamic_slice_in_dim(step_count, ens_index * members_dev, members_dev)
    counts = jnp.broadcast_to(
        own_counts.reshape(members_dev // sub, sub, 1), (members_dev // sub, sub, lane)
    )
    bb = jnp.stack([base_thickness, balance], axis=1)
    thickness, gathered = advance(params, bb, counts, lax.axis_size("space"), enss)
    tile_cells = params.shape[1] * params.shape[2]
    predicted = jnp.take(thickness.reshape(members_dev, tile_cells), obs_index, axis=1)
    obs_block = lax.all_to_all(predicted, "ens", split_axis=1, concat_axis=0, tiled=True)
    block_width = obs_block.shape[1]
    observed_part = lax.dynamic_slice_in_dim(observed, ens_index * block_width, block_width)
    noise_part = lax.dynamic_slice_in_dim(noise_var, ens_index * block_width, block_width)
    gram, cross = ensemble_terms(obs_block, observed_part, noise_part)
    gram, cross = lax.psum((gram, cross), ("space", "ens"))
    weights = solve_weights(gram, cross)
    weight_cols = lax.dynamic_slice_in_dim(weights, ens_index * members_dev, members_dev, 1)
    flat_piece = gathered.reshape(members, tile_cells)
    weighted = jnp.dot(weight_cols.T, flat_piece, precision=lax.Precision.HIGHEST)
    member_total = jnp.sum(flat_piece, axis=0)
    column_sums = jnp.sum(weight_cols, axis=0)
    increment = weighted - column_sums[:, None] * member_total[None, :] / members
    updated = params + increment.reshape(params.shape)
    return (thickness, updated)


def solution(mesh):
    in_specs = (
        P("ens", "space", None),
        P("space", None),
        P("space", None),
        P(),
        P("space"),
        P("space"),
        P("space"),
    )
    out_specs = (P("ens", "space", None), P("ens", "space", None))
    return jax.shard_map(shards, mesh=mesh, in_specs=in_specs, out_specs=out_specs, check_vma=False)
```

time: 566 us -> 257 us (0.45)
  starting transfers between devices: 242 us -> 3.26 us
  Pallas kernels: 0 us -> 174 us
  other arithmetic: 136 us -> 15.7 us
  local copies, waits for them, and re-layouts: 57.3 us -> 13.7 us
  waiting for transfers between devices: 35.1 us -> 1.02 us
  loops' own time: 21.8 us -> 0 us
  between operations: 14.3 us -> 0.81 us
  blocking collectives: 50.6 us -> 44.3 us
    ppermute x66 -> x0, starting transfers between devices: 238 us -> none  [the longest x33 196 us: padded_2(): lax.ppermute(lax.slice_in_dim(block, block.shape[dim] - width, None, axis...]
    pallas_call x0 -> x1, Pallas kernels: none -> 174 us  [advance(): pl.pallas_call(functools.partial(advance_kernel, spaces, enss), out_shape...]
    select_n x32 -> x0, other arithmetic: 87.3 us -> none  [advance(): return jnp.where((step_index < own_counts)[:, None, None], moved, thickness)]
    while x33 -> x0, local copies, waits for them, and re-layouts: 43 us -> none
    div x32 -> x0, other arithmetic: 32.8 us -> none  [stencil(): diffusivity = slip_padded * padded * padded / (1.0 + padded * padded)]
    ppermute x66 -> x0, waiting for transfers between devices: 30.6 us -> none  [the longest x33 27.4 us: padded_2(): lax.ppermute(lax.slice_in_dim(block, block.shape[dim] - width, None, axis...]
    another operation x1 -> x0, loops' own time: 21.8 us -> none  [shards(): thickness = lax.fori_loop(0, longest, advance, initial)]
    psum x1, blocking collectives: 50.6 us -> 44.3 us  [shards(): gram, cross = lax.psum((gram, cross), ('space', 'ens'))]
  transfers between devices with their start and end apart: 68 -> 1, of which waited for: 34 -> 1; matrix products, arithmetic and copies ran while one was open for 34% -> 1% of each run, Pallas kernels for 0% -> 0%
where the time goes in v1:
time: 257 us; the launch traced here: 256 us
  Pallas kernels  174 us (68%)
  blocking collectives  44.3 us (17%)
  other arithmetic  15.7 us (6%)
  local copies, waits for them, and re-layouts  13.7 us (5%)
  matrix products  3.68 us (1%)
  starting transfers between devices  3.26 us (1%)
    pallas_call x1, Pallas kernels, advance(): pl.pallas_call(functools.partial(advance_kernel, spaces, enss), out_shape...  174 us
    psum x1, blocking collectives, shards(): gram, cross = lax.psum((gram, cross), ('space', 'ens'))  44.3 us
    another operation x3, other arithmetic, solve_weights(): factor = jnp.linalg.cholesky(gram + jnp.eye(members, dtype=gram.dtype))  6.52 us
    another operation x2, other arithmetic, solve_weights(): lax.linalg.triangular_solve(factor, inner, left_side=True, lower=True, tr...  5.55 us
    unnamed x12, local copies, waits for them, and re-layouts  5.42 us
  transfers between devices with their start and end apart: 1, of which 1 were waited for; matrix products, arithmetic and copies ran while one was open for 1% of the time, Pallas kernels for 0%

profile of v1, /device:TPU:0, one launch (start us, length us, event | category | flops | bytes accessed | tf_op | source)
XLA Modules:
  0.0 256.4 jit_solution(4981221391300487704)
XLA Ops:
  0.6 0.7 compare_select_fusion
  1.3 0.7 and_bitcast_fusion
  2.0 0.7 dynamic_slice.12
  2.7 0.1 broadcast_in_dim.29
  2.8 0.8 stack.10
  3.6 0.8 stack.9
  4.4 0.1 pad_maximum_fusion.bb_ref
  4.5 0.1 broadcast_in_dim.30.count_ref
  4.5 0.0 copy-start
  4.5 1.2 copy-done
  5.8 173.9 %advance.1 = (f32[32,16,512]{2,1,0:T(8,128)S(1)}, f32[2,32,16,512]{3,2,1,0:T(8,128)S(1)}) custom-call(f32[32,16,512]{2,1,0:T(8,128)S(1)} %copy-done, f32[32,16,512]{2,1,0:T(8,128)S(1)} %copy-done, f32[16,2,512]{2,1,0:T(2,128)S(1)} %pad_maximum_fusion.bb_ref, s32[4,8,128]{2,1,0:T(8,128)S(1)} %broadcast_in_dim.30.count_ref), custom_call_target="tpu_custom_call" | custom-call | tf_op jit(solution)/shard_map/advance/pallas_call | solution.py:257
  179.6 0.0 copy-start.2
  179.7 0.0 copy-start.3
  179.7 2.6 %copy.14 = f32[32,16,512]{0,2,1:T(8,128)} copy(f32[32,16,512]{2,1,0:T(8,128)S(1)} %get-tuple-element.12) | data formatting | bytes 2097152 | tf_op jit(solution)/shard_map/reshape | solution.py:321
  182.3 2.9 %gather_fusion = f32[256,32]{1,0:T(8,128)S(1)} fusion(f32[32,8192]{0,1:T(8,128)} %bitcast.40, s32[1024]{0:T(1024)S(1)} %pad_clamp_fusion), kind=kCustom, calls=%fused_computation | custom fusion | bytes 66560 | tf_op jit(solution)/shard_map/jit(_take)/gather | solution.py:321
  185.2 0.1 copy.12
  185.3 0.6 broadcast_select_fusion
  185.9 3.3 %all-to-all-start = ((f32[32,2,128]{2,0,1:T(8,128)}), f32[32,2,128]{2,0,1:T(8,128)S(1)}, u32[]{:S(2)}, u32[]{:S(2)}) async-start(f32[32,2,128]{2,0,1:T(8,128)} %broadcast_select_fusion), calls=%async_computation | async-start | bytes 65536 | tf_op jit(solution)/shard_map/all_to_all | solution.py:322
  189.2 0.0 copy-done.2
  189.2 0.1 dynamic-slice_rsqrt_fusion
  189.3 0.0 copy-done.3
  189.3 0.1 dynamic_slice.14
  189.4 2.6 %copy.15 = f32[8,8,16,512]{3,1,2,0:T(8,128)} copy(f32[8,8,16,512]{3,2,1,0:T(8,128)S(1)} %bitcast.38) | data formatting | bytes 4194304
  191.9 0.1 reduce_sum.29
  192.1 1.0 all-to-all-done
  193.2 0.2 fusion.10
  193.3 0.2 fusion.11
  193.5 44.3 %all-reduce = (f32[64,64]{1,0:T(8,128)S(1)}, f32[64,64]{1,0:T(8,128)S(1)}) all-reduce(f32[64,64]{1,0:T(8,128)S(1)} %fusion.11, f32[64,64]{1,0:T(8,128)S(1)} %fusion.10), channel_id=1, replica_groups=mesh['space'=16,'ens'=2] {'space','ens'}, use_global_device_ids=true, to_apply=%region_4.5 | all-reduce | flops 8192 | bytes 65536 | tf_op jit(solution)/shard_map/psum | solution.py:327
  237.9 0.1 copy.13
  238.0 5.8 %cholesky.17 = f32[64,64]{1,0:T(8,128)S(1)} custom-call(f32[64,64]{1,0:T(8,128)S(1)} %fusion.5), custom_call_target="Cholesky" | custom-call | tf_op jit(solution)/shard_map/jit(cholesky)/cholesky | solution.py:301
  243.9 0.6 compare_reduce_fusion
  244.5 0.7 fusion
  245.2 4.9 %custom-call.8 = f32[1,64,64]{1,2,0:T(8,128)S(1)} custom-call(f32[1,64,64]{2,1,0:T(8,128)S(1)} %fusion), custom_call_target="InvertDiagBlocksLowerTriangular" | custom-call | tf_op jit(solution)/shard_map/triangular_solve | solution.py:303
  250.1 0.3 fusion.3
  250.4 0.2 fusion.1
  250.6 0.1 fusion.6
  250.7 0.0 copy-start.1
  250.7 2.8 %convolution_subtract_fusion = f32[32,8192]{1,0:T(8,128)S(1)} fusion(f32[64,8192]{1,0:T(8,128)} %bitcast.39, f32[8192]{0:T(1024)S(1)} %bitcast.45, f32[32]{0:T(128)S(1)} %fusion.6, f32[64,64]{0,1:T(8,128)S(1)} %fusion.1, s32[]{:T(128)S(6)} %select_n.22), kind=kOutput, calls=%fused_computation.1 | convolution fusion | flops 202115072 | bytes 3195396 | tf_op jit(solution)/shard_map/dot_general | solution.py:331
  253.6 0.6 copy.17
  254.2 0.0 copy-done.1
  254.2 1.2 bitcast_add_fusion
  255.4 1.0 copy.19
  (8 shorter events, 0.1 us)
Async XLA Ops:
  4.5 1.2 copy-start
  179.6 9.5 %copy-start.2 = (f32[256]{0:T(256)S(1)}, f32[256]{0:T(256)}, u32[]{:S(2)}) copy-start(f32[256]{0:T(256)} %param.13) | copy-start | bytes 3076
  179.7 9.6 %copy-start.3 = (f32[256]{0:T(256)S(1)}, f32[256]{0:T(256)}, u32[]{:S(2)}) copy-start(f32[256]{0:T(256)} %param.12) | copy-start | bytes 3076
  185.9 7.2 %all-to-all-start = ((f32[32,2,128]{2,0,1:T(8,128)}), f32[32,2,128]{2,0,1:T(8,128)S(1)}, u32[]{:S(2)}, u32[]{:S(2)}) async-start(f32[32,2,128]{2,0,1:T(8,128)} %broadcast_select_fusion), calls=%async_computation | async-start | bytes 65536 | tf_op jit(solution)/shard_map/all_to_all | solution.py:322
  250.7 3.5 %copy-start.1 = (f32[32,16,512]{2,1,0:T(8,128)S(1)}, f32[32,16,512]{2,1,0:T(8,128)}, u32[]{:S(2)}) copy-start(f32[32,16,512]{2,1,0:T(8,128)} %params_any.1) | copy-start | bytes 3145732

commit v2 on v1

--- a/solution.py
+++ b/solution.py
@@ -8,7 +8,7 @@
 
 time_step = 0.11
 steps = 32
-halo = 4
+halo = 1
 sub = 8
 lane = 128
 MESH = pl.DeviceIdType.MESH
@@ -17,6 +17,13 @@
 def reciprocal(x):
     r = pl.reciprocal(x, approx=True)
     return r * (2.0 - x * r)
+
+
+def dot(left, right, right_dim):
+    return lax.dot_general(
+        left, right, (((1,), (right_dim,)), ((), ())),
+        precision=lax.Precision.HIGHEST, preferred_element_type=jnp.float32,
+    )
 
 
 def substep(h_ref, slip_ref, bal_ref, group, first, last, masks, rows):
@@ -59,9 +66,10 @@
 
 
 def advance_kernel(
-    spaces, enss, params_ref, params_any, bb_ref, count_ref, out_ref, gathered,
-    h_ref, slip_ref, bal_ref, land_ref, bb_land,
-    send_sem, recv_sem, slip_send, slip_recv, bb_send, bb_recv, ens_send, ens_recv, own_sem,
+    spaces, enss, params_ref, bb_ref, count_ref, cell_ref, observed_ref, noise_ref, out_ref, updated_ref,
+    h_ref, slip_ref, bal_ref, land_ref, bb_land, par_ref, pred_ref, sum_ref, sum_land,
+    send_sem, recv_sem, slip_send, slip_recv, bb_send, bb_recv, ens_send, ens_recv,
+    pred_send, pred_recv, sum_send, sum_recv,
 ):
     members, rows, width = params_ref.shape
     groups = members // sub
@@ -74,6 +82,11 @@
     up = jnp.maximum(me - 1, 0)
     down = jnp.minimum(me + 1, spaces - 1)
     others = [lax.rem(ens + step, enss) for step in range(1, enss)]
+    stages = spaces.bit_length() - 1
+    partners = []
+    for stage in range(stages):
+        bit = 1 << stage
+        partners.append(me + bit - 2 * bit * lax.rem(lax.div(me, bit), 2))
 
     barrier = pltpu.get_barrier_semaphore()
 
@@ -87,7 +100,9 @@
 
     for other in others:
         pl.semaphore_signal(barrier, inc=1, device_id={"ens": other}, device_id_type=MESH)
-    neighbours = has_up.astype(jnp.int32) + has_down.astype(jnp.int32) + (enss - 1)
+    for partner in partners:
+        pl.semaphore_signal(barrier, inc=1, device_id={"space": partner}, device_id_type=MESH)
+    neighbours = has_up.astype(jnp.int32) + has_down.astype(jnp.int32) + (enss - 1) + stages
     pl.semaphore_wait(barrier, neighbours)
 
     sides = (
@@ -150,24 +165,24 @@
 
     @pl.loop(0, groups)
     def _(group):
-        block = params_ref[pl.ds(group * sub, sub)]
-        turned = jnp.swapaxes(jnp.exp(block) * (0.5 * time_step), 0, 1)
-        slip_ref[group, pl.ds(halo, rows)] = turned
+        turned = jnp.swapaxes(params_ref[pl.ds(group * sub, sub)], 0, 1)
+        par_ref[ens * groups + group] = turned
+        slip_ref[group, pl.ds(halo, rows)] = jnp.exp(turned) * (0.5 * time_step)
         for side in range(2):
             @pl.when(sides[side][0])
             def _(side=side):
                 slip_copy(group, side).start()
 
+    own_groups = pl.ds(ens * groups, groups)
+
     def ens_copy(step):
         return pltpu.make_async_remote_copy(
-            params_any, gathered.at[ens], ens_send.at[step], ens_recv.at[step],
+            par_ref.at[own_groups], par_ref.at[own_groups], ens_send.at[step], ens_recv.at[step],
             device_id={"ens": others[step]}, device_id_type=MESH,
         )
 
     for step in range(enss - 1):
         ens_copy(step).start()
-    own_copy = pltpu.make_async_copy(params_ref, gathered.at[ens], own_sem)
-    own_copy.start()
 
     def wide(row):
         return jnp.broadcast_to(row, (sub, width))
@@ -233,41 +248,120 @@
                 def _(side=side):
                     h_copy(group, side, 1 - slot).start()
 
+    for side in range(2):
+        @pl.when(sides[side][0])
+        def _(side=side):
+            for group in range(groups):
+                slip_copy(group, side).wait_send()
+
+    cell_row = cell_ref[0:1, :]
+    cell_col = cell_ref[1:2, :]
+    count_obs = cell_ref.shape[1]
+    one_hot = jnp.where(
+        lax.broadcasted_iota(jnp.int32, (width, count_obs), 0) == cell_col, 1.0, 0.0
+    )
+    at_row = lax.broadcasted_iota(jnp.int32, (rows, sub, count_obs), 0) == cell_row
+    for group in range(groups):
+        cells = h_ref[group, pl.ds(halo, rows)].reshape(rows * sub, width)
+        picked = dot(cells, one_hot, 0).reshape(rows, sub, count_obs)
+        pred_ref[ens, pl.ds(group * sub, sub)] = jnp.sum(jnp.where(at_row, picked, 0.0), axis=0)
+
+    def pred_copy(step):
+        return pltpu.make_async_remote_copy(
+            pred_ref.at[ens], pred_ref.at[ens], pred_send.at[step], pred_recv.at[step],
+            device_id={"ens": others[step]}, device_id_type=MESH,
+        )
+
+    for step in range(enss - 1):
+        pred_copy(step).start()
     for group in range(groups):
         out_ref[pl.ds(group * sub, sub)] = jnp.swapaxes(h_ref[group, pl.ds(halo, rows)], 0, 1)
-
-    own_copy.wait()
+    for step in range(enss - 1):
+        pred_copy(step).wait()
+
+    every = enss * members
+    scaling = lax.rsqrt(noise_ref[...])
+    predicted = pred_ref[...].reshape(every, count_obs)
+    average = jnp.sum(predicted, axis=0, keepdims=True) * (1.0 / every)
+    root = jnp.sqrt(jnp.float32(every - 1))
+    anomalies = (predicted - average) * (scaling / root)
+    mismatch = (observed_ref[...] - pred_ref[ens]) * scaling
+    spread = sum_ref.shape[2]
+    filler = jnp.zeros((spread - every - members, count_obs), jnp.float32)
+    sum_ref[0] = dot(anomalies, jnp.concatenate([anomalies, mismatch, filler], axis=0), 1)
+
+    def sum_copy(stage):
+        return pltpu.make_async_remote_copy(
+            sum_ref.at[stage], sum_land.at[stage], sum_send.at[stage], sum_recv.at[stage],
+            device_id={"space": partners[stage]}, device_id_type=MESH,
+        )
+
+    for stage in range(stages):
+        sum_copy(stage).start()
+        sum_copy(stage).wait_recv()
+        sum_ref[stage + 1] = sum_ref[stage] + sum_land[stage]
+
+    row_of = lax.broadcasted_iota(jnp.int32, (every, spread), 0)
+    lane_of = lax.broadcasted_iota(jnp.int32, (every, spread), 1)
+    system = sum_ref[stages] + jnp.where(row_of == lane_of, 1.0, 0.0)
+    for pivot in range(every):
+        column = system[:, pivot : pivot + 1]
+        row = system[pivot : pivot + 1, :]
+        row = row / row[:, pivot : pivot + 1]
+        system = jnp.where(row_of == pivot, row, system - column * row)
+    weights = system[:, every : every + members] / root
+    weights = weights - jnp.sum(weights, axis=0, keepdims=True) * (1.0 / every)
+    weights = weights.T
+
     for step in range(enss - 1):
         ens_copy(step).wait()
+
+    @pl.loop(0, rows)
+    def _(row):
+        block = par_ref[:, row].reshape(every, width)
+        own = par_ref[own_groups, row]
+        slip_ref[:, row] = own + dot(weights, block, 0).reshape(groups, sub, width)
+
+    for group in range(groups):
+        updated_ref[pl.ds(group * sub, sub)] = jnp.swapaxes(slip_ref[group, pl.ds(0, rows)], 0, 1)
+
+    for stage in range(stages):
+        sum_copy(stage).wait_send()
     for side in range(2):
         @pl.when(sides[side][0])
         def _(side=side):
             bb_copy(side).wait_send()
-            for group in range(groups):
-                slip_copy(group, side).wait_send()
-
-
-def advance(params, bb, counts, spaces, enss):
+
+
+def advance(params, bb, counts, cells, observed, noise_var, spaces, enss):
     members, rows, width = params.shape
     groups = members // sub
     total = rows + 2 * halo
+    every = members * enss
+    count_obs = cells.shape[1]
+    spread = pl.cdiv(every + members, lane) * lane
+    stages = spaces.bit_length() - 1
+    assert 1 << stages == spaces
     dma = pltpu.SemaphoreType.DMA
     vmem = pl.BlockSpec(memory_space=pltpu.VMEM)
-    hbm = pl.BlockSpec(memory_space=pl.ANY)
     return pl.pallas_call(
         functools.partial(advance_kernel, spaces, enss),
         out_shape=(
             jax.ShapeDtypeStruct(params.shape, jnp.float32),
-            jax.ShapeDtypeStruct((enss, members, rows, width), jnp.float32),
+            jax.ShapeDtypeStruct(params.shape, jnp.float32),
         ),
-        in_specs=[vmem, hbm, vmem, vmem],
-        out_specs=(vmem, hbm),
+        in_specs=[vmem] * 6,
+        out_specs=(vmem, vmem),
         scratch_shapes=[
             pltpu.VMEM((groups, total, sub, width), jnp.float32),
             pltpu.VMEM((groups, total, sub, width), jnp.float32),
             pltpu.VMEM((total, sub, width), jnp.float32),
             pltpu.VMEM((groups, 2, 2, halo, sub, width), jnp.float32),
             pltpu.VMEM((2, halo, 2, width), jnp.float32),
+            pltpu.VMEM((enss * groups, rows, sub, width), jnp.float32),
+            pltpu.VMEM((enss, members, count_obs), jnp.float32),
+            pltpu.VMEM((stages + 1, every, spread), jnp.float32),
+            pltpu.VMEM((stages, every, spread), jnp.float32),
             dma((groups, 2)),
             dma((groups, 2, 2)),
             dma((groups, 2)),
@@ -276,64 +370,31 @@
             dma((2,)),
             dma((max(enss - 1, 1),)),
             dma((max(enss - 1, 1),)),
-            dma(()),
+            dma((max(enss - 1, 1),)),
+            dma((max(enss - 1, 1),)),
+            dma((stages,)),
+            dma((stages,)),
         ],
         compiler_params=pltpu.CompilerParams(
             collective_id=0, has_side_effects=True, vmem_limit_bytes=40 * 1024 * 1024
         ),
         name="advance",
-    )(params, params, bb, counts)
-
-
-def ensemble_terms(predicted, observed, noise_var):
-    members = predicted.shape[0]
-    scaling = lax.rsqrt(noise_var)
-    average = jnp.mean(predicted, axis=0)
-    anomalies = (predicted - average) * scaling / jnp.sqrt(jnp.float32(members - 1))
-    mismatch = (observed - predicted) * scaling
-    gram = jnp.dot(anomalies, anomalies.T, precision=lax.Precision.HIGHEST)
-    cross = jnp.dot(anomalies, mismatch.T, precision=lax.Precision.HIGHEST)
-    return (gram, cross)
-
-
-def solve_weights(gram, cross):
-    members = gram.shape[0]
-    factor = jnp.linalg.cholesky(gram + jnp.eye(members, dtype=gram.dtype))
-    inner = lax.linalg.triangular_solve(factor, cross, left_side=True, lower=True)
-    result = lax.linalg.triangular_solve(
-        factor, inner, left_side=True, lower=True, transpose_a=True
-    )
-    return result / jnp.sqrt(jnp.float32(members - 1))
+    )(params, bb, counts, cells, observed, noise_var)
 
 
 def shards(params, base_thickness, balance, step_count, obs_index, observed, noise_var):
     members_dev = params.shape[0]
     ens_index = lax.axis_index("ens")
     enss = lax.axis_size("ens")
-    members = members_dev * enss
     own_counts = lax.dynamic_slice_in_dim(step_count, ens_index * members_dev, members_dev)
     counts = jnp.broadcast_to(
         own_counts.reshape(members_dev // sub, sub, 1), (members_dev // sub, sub, lane)
     )
     bb = jnp.stack([base_thickness, balance], axis=1)
-    thickness, gathered = advance(params, bb, counts, lax.axis_size("space"), enss)
-    tile_cells = params.shape[1] * params.shape[2]
-    predicted = jnp.take(thickness.reshape(members_dev, tile_cells), obs_index, axis=1)
-    obs_block = lax.all_to_all(predicted, "ens", split_axis=1, concat_axis=0, tiled=True)
-    block_width = obs_block.shape[1]
-    observed_part = lax.dynamic_slice_in_dim(observed, ens_index * block_width, block_width)
-    noise_part = lax.dynamic_slice_in_dim(noise_var, ens_index * block_width, block_width)
-    gram, cross = ensemble_terms(obs_block, observed_part, noise_part)
-    gram, cross = lax.psum((gram, cross), ("space", "ens"))
-    weights = solve_weights(gram, cross)
-    weight_cols = lax.dynamic_slice_in_dim(weights, ens_index * members_dev, members_dev, 1)
-    flat_piece = gathered.reshape(members, tile_cells)
-    weighted = jnp.dot(weight_cols.T, flat_piece, precision=lax.Precision.HIGHEST)
-    member_total = jnp.sum(flat_piece, axis=0)
-    column_sums = jnp.sum(weight_cols, axis=0)
-    increment = weighted - column_sums[:, None] * member_total[None, :] / members
-    updated = params + increment.reshape(params.shape)
-    return (thickness, updated)
+    cells = jnp.stack([obs_index // params.shape[2], obs_index % params.shape[2]])
+    return advance(
+        params, bb, counts, cells, observed[None], noise_var[None], lax.axis_size("space"), enss
+    )
 
 
 def solution(mesh):

time: 257 us -> 139 us (0.54)
  blocking collectives: 44.3 us -> 0 us
  Pallas kernels: 174 us -> 132 us
  other arithmetic: 15.7 us -> 0.76 us
  local copies, waits for them, and re-layouts: 13.7 us -> 5.44 us
  matrix products: 3.68 us -> 0 us
  starting transfers between devices: 3.26 us -> 0 us
    psum x1 -> x0, blocking collectives: 44.3 us -> none  [shards(): gram, cross = lax.psum((gram, cross), ('space', 'ens'))]
    pallas_call x1, Pallas kernels: 174 us -> 132 us  [advance(): pl.pallas_call(functools.partial(advance_kernel, spaces, enss), out_shape...]
    another operation x5 -> x1, other arithmetic: 12.1 us -> 0.01 us  [shards(): jnp.stack([obs_index // params.shape[2], obs_index % params.shape[2]])]
    all_to_all x1 -> x0, starting transfers between devices: 3.26 us -> none  [shards(): lax.all_to_all(predicted, 'ens', split_axis=1, concat_axis=0, tiled=True)]
    dot_general x3 -> x0, matrix products: 3.19 us -> none  [the longest x1 2.83 us: shards(): jnp.dot(weight_cols.T, flat_piece, precision=lax.Precision.HIGHEST)]
    gather x2 -> x0, local copies, waits for them, and re-layouts: 2.97 us -> none  [shards(): jnp.take(thickness.reshape(members_dev, tile_cells), obs_index, axis=1)]
    reshape x1 -> x0, local copies, waits for them, and re-layouts: 2.64 us -> none  [shards(): thickness.reshape(members_dev, tile_cells)]
  transfers between devices with their start and end apart: 1 -> 0, of which waited for: 1 -> 0; matrix products, arithmetic and copies ran while one was open for 1% -> 0% of each run, Pallas kernels for 0% -> 0%
where the time goes in v2:
time: 139 us
  Pallas kernels  132 us (95%)
  local copies, waits for them, and re-layouts  5.44 us (4%)
    pallas_call x1, Pallas kernels, advance(): pl.pallas_call(functools.partial(advance_kernel, spaces, enss), out_shape...  132 us
    unnamed x12, local copies, waits for them, and re-layouts  4.51 us

profile of v2, /device:TPU:0, one launch (start us, length us, event | category | flops | bytes accessed | tf_op | source)
XLA Modules:
  0.0 138.7 jit_solution(13001824888540434268)
XLA Ops:
  0.6 0.0 copy-start.3
  0.6 0.7 dynamic_slice.3
  1.4 0.1 broadcast_in_dim.13
  1.5 0.7 and_select_fusion.1
  2.2 0.1 broadcast_in_dim.14.count_ref
  2.2 0.0 copy-done.3
  2.2 0.0 copy-start.4
  2.3 0.7 copy-done.4
  3.0 0.0 copy-start.1
  3.0 0.0 copy-start.2
  3.0 0.1 pad_maximum_fusion.bb_ref
  3.1 0.6 copy-done.1
  3.7 0.0 copy-done.2
  3.7 0.0 copy-start
  3.7 1.2 copy-done
  4.9 131.8 %advance.1 = (f32[32,16,512]{2,1,0:T(8,128)S(1)}, f32[32,16,512]{2,1,0:T(8,128)S(1)}) custom-call(f32[32,16,512]{2,1,0:T(8,128)S(1)} %copy-done, f32[16,2,512]{2,1,0:T(2,128)S(1)} %pad_maximum_fusion.bb_ref, s32[4,8,128]{2,1,0:T(8,128)S(1)} %broadcast_in_dim.14.count_ref, s32[2,256]{1,0:T(2,128)S(1)} %pad_add_fusion.cell_ref, f32[1,256]{1,0:T(1,128)S(1)} %bitcast.4, ...), custom_call_target="tpu_custom_call" | custom-call | tf_op jit(solution)/shard_map/advance/pallas_call | solution.py:347
  136.8 1.0 copy.11
  137.8 1.0 copy.12
  (3 shorter events, 0.1 us)
Async XLA Ops:
  0.6 1.6 %copy-start.3 = (f32[16,512]{1,0:T(8,128)S(1)}, f32[16,512]{1,0:T(8,128)}, u32[]{:S(2)}) copy-start(f32[16,512]{1,0:T(8,128)} %param.8) | copy-start | bytes 98308
  2.2 0.8 copy-start.4
  3.0 0.7 copy-start.1
  3.0 0.7 copy-start.2
  3.7 1.2 copy-start

commit v3 on v2

--- a/solution.py
+++ b/solution.py
@@ -8,7 +8,7 @@
 
 time_step = 0.11
 steps = 32
-halo = 1
+halo = 2
 sub = 8
 lane = 128
 MESH = pl.DeviceIdType.MESH
@@ -32,7 +32,6 @@
     at_end = lanes == lane - 1
     at_start = lanes == 0
     cols = [pl.ds(p * lane, lane) for p in range(pieces)]
-    zero = jnp.zeros((sub, lane), jnp.float32)
     prev = None
     for row in range(first, last):
         h = [h_ref[group, row, :, c] for c in cols]
@@ -46,17 +45,14 @@
             if prev_down is not None:
                 out = row - 1
                 mask = masks[0] if out < halo else masks[1] if out < halo + rows else masks[2]
-                h_rot = [pltpu.roll(prev_h[p], lane - 1, 1) for p in range(pieces)] + [zero]
-                d_rot = [pltpu.roll(prev_d[p], lane - 1, 1) for p in range(pieces)] + [zero]
-                flux = []
-                for p in range(pieces):
-                    h_right = jnp.where(at_end, h_rot[p + 1], h_rot[p])
-                    d_right = jnp.where(at_end, d_rot[p + 1], d_rot[p])
-                    flux.append((d_right + prev_d[p]) * (h_right - prev_h[p]))
-                f_rot = [pltpu.roll(flux[p], 1, 1) for p in range(pieces)]
+                h_next = prev_h[1:] + [jnp.where(at_end, 0.0, pltpu.roll(prev_h[0], lane - 1, 1))]
+                d_next = prev_d[1:] + [jnp.where(at_end, 0.0, pltpu.roll(prev_d[0], lane - 1, 1))]
+                flux = [
+                    (d_next[p] + prev_d[p]) * (h_next[p] - prev_h[p]) for p in range(pieces)
+                ]
+                edge = jnp.where(at_start, prev_d[0] * prev_h[0], pltpu.roll(flux[-1], 1, 1))
                 for p, c in enumerate(cols):
-                    edge = prev_d[0] * prev_h[0] if p == 0 else f_rot[p - 1]
-                    f_left = jnp.where(at_start, edge, f_rot[p])
+                    f_left = edge if p == 0 else flux[p - 1]
                     change = (down[p] - prev_down[p]) + (flux[p] - f_left)
                     moved = (prev_h[p] + bal_ref[out, :, c]) + change
                     h_ref[group, out, :, c] = jnp.where(mask, moved, prev_h[p])
@@ -67,7 +63,7 @@
 
 def advance_kernel(
     spaces, enss, params_ref, bb_ref, count_ref, cell_ref, observed_ref, noise_ref, out_ref, updated_ref,
-    h_ref, slip_ref, bal_ref, land_ref, bb_land, par_ref, pred_ref, sum_ref, sum_land,
+    h_ref, slip_ref, bal_ref, land_ref, bb_land, par_ref, pred_ref, sum_ref, sum_land, order_ref,
     send_sem, recv_sem, slip_send, slip_recv, bb_send, bb_recv, ens_send, ens_recv,
     pred_send, pred_recv, sum_send, sum_recv,
 ):
@@ -88,6 +84,14 @@
         bit = 1 << stage
         partners.append(me + bit - 2 * bit * lax.rem(lax.div(me, bit), 2))
 
+    pieces = width // lane
+    column_of = lax.broadcasted_iota(jnp.int32, (width, lane), 0)
+    first_of = lax.broadcasted_iota(jnp.int32, (width, lane), 1) * pieces
+    for piece in range(pieces):
+        order_ref[:, piece * lane : (piece + 1) * lane] = jnp.where(
+            column_of == first_of + piece, 1.0, 0.0
+        )
+
     barrier = pltpu.get_barrier_semaphore()
 
     @pl.when(has_up)
@@ -167,7 +171,8 @@
     def _(group):
         turned = jnp.swapaxes(params_ref[pl.ds(group * sub, sub)], 0, 1)
         par_ref[ens * groups + group] = turned
-        slip_ref[group, pl.ds(halo, rows)] = jnp.exp(turned) * (0.5 * time_step)
+        slip = (jnp.exp(turned) * (0.5 * time_step)).reshape(rows * sub, width)
+        slip_ref[group, pl.ds(halo, rows)] = dot(slip, order_ref[...], 0).reshape(rows, sub, width)
         for side in range(2):
             @pl.when(sides[side][0])
             def _(side=side):
@@ -238,10 +243,11 @@
             counts = (
                 count * has_up.astype(jnp.int32), count, count * has_down.astype(jnp.int32)
             )
-            for step in range(halo):
+            @pl.loop(0, halo)
+            def _(step):
                 now = block * halo + step
                 masks = [now < value for value in counts]
-                substep(h_ref, slip_ref, bal_ref, group, step, total - step, masks, rows)
+                substep(h_ref, slip_ref, bal_ref, group, 0, total, masks, rows)
 
             for side in range(2):
                 @pl.when(jnp.logical_and(sides[side][0], block < blocks - 1))
@@ -275,7 +281,9 @@
     for step in range(enss - 1):
         pred_copy(step).start()
     for group in range(groups):
-        out_ref[pl.ds(group * sub, sub)] = jnp.swapaxes(h_ref[group, pl.ds(halo, rows)], 0, 1)
+        cells = h_ref[group, pl.ds(halo, rows)].reshape(rows * sub, width)
+        ordered = dot(cells, order_ref[...], 1).reshape(rows, sub, width)
+        out_ref[pl.ds(group * sub, sub)] = jnp.swapaxes(ordered, 0, 1)
     for step in range(enss - 1):
         pred_copy(step).wait()
 
@@ -362,6 +370,7 @@
             pltpu.VMEM((enss, members, count_obs), jnp.float32),
             pltpu.VMEM((stages + 1, every, spread), jnp.float32),
             pltpu.VMEM((stages, every, spread), jnp.float32),
+            pltpu.VMEM((width, width), jnp.float32),
             dma((groups, 2)),
             dma((groups, 2, 2)),
             dma((groups, 2)),
@@ -391,7 +400,11 @@
         own_counts.reshape(members_dev // sub, sub, 1), (members_dev // sub, sub, lane)
     )
     bb = jnp.stack([base_thickness, balance], axis=1)
-    cells = jnp.stack([obs_index // params.shape[2], obs_index % params.shape[2]])
+    rows, width = base_thickness.shape
+    pieces = width // lane
+    bb = bb.reshape(rows, 2, lane, pieces).swapaxes(2, 3).reshape(rows, 2, width)
+    column = obs_index % width
+    cells = jnp.stack([obs_index // width, column % pieces * lane + column // pieces])
     return advance(
         params, bb, counts, cells, observed[None], noise_var[None], lax.axis_size("space"), enss
     )

time: 139 us -> 93.3 us (0.67)
  Pallas kernels: 132 us -> 86.8 us
    pallas_call x1, Pallas kernels: 132 us -> 86.8 us  [advance(): pl.pallas_call(functools.partial(advance_kernel, spaces, enss), out_shape...]
where the time goes in v3:
time: 93.3 us; the launch traced here: 93 us
  Pallas kernels  86.8 us (93%)
  local copies, waits for them, and re-layouts  4.85 us (5%)
    pallas_call x1, Pallas kernels, advance(): pl.pallas_call(functools.partial(advance_kernel, spaces, enss), out_shape...  86.8 us
    unnamed x12, local copies, waits for them, and re-layouts  3.59 us

profile of v3, /device:TPU:0, one launch (start us, length us, event | category | flops | bytes accessed | tf_op | source)
XLA Modules:
  0.0 93.0 jit_solution(9338570175234746733)
XLA Ops:
  0.6 0.0 copy-start.3
  0.6 0.0 copy-start
  0.7 0.8 dynamic_slice.3
  1.5 0.1 broadcast_in_dim.13
  1.6 0.7 and_select_fusion.3
  2.3 0.1 broadcast_in_dim.14.count_ref
  2.3 0.0 copy-done.3
  2.3 0.1 copy.14
  2.5 0.1 copy.16
  2.6 0.9 copy.15
  3.5 0.1 copy.17
  3.6 0.1 copy.18
  3.6 0.0 copy-start.1
  3.6 0.0 copy-start.2
  3.7 0.1 reshape.14.bb_ref
  3.7 0.0 copy-done
  3.7 0.6 copy-done.1
  4.3 0.0 copy-done.2
  4.3 86.8 %advance.1 = (f32[32,16,512]{2,1,0:T(8,128)S(1)}, f32[32,16,512]{2,1,0:T(8,128)S(1)}) custom-call(f32[32,16,512]{2,1,0:T(8,128)S(1)} %copy-done, f32[16,2,512]{2,1,0:T(2,128)S(1)} %reshape.14.bb_ref, s32[4,8,128]{2,1,0:T(8,128)S(1)} %broadcast_in_dim.14.count_ref, s32[2,256]{1,0:T(2,128)S(1)} %pad_add_fusion.cell_ref, f32[1,256]{1,0:T(1,128)S(1)} %bitcast.8, ...), custom_call_target="tpu_custom_call" | custom-call | tf_op jit(solution)/shard_map/advance/pallas_call | solution.py:355
  91.1 1.0 %copy.21 = f32[32,16,512]{2,1,0:T(8,128)} copy(f32[32,16,512]{2,1,0:T(8,128)S(1)} %get-tuple-element.6) | data formatting | bytes 2097152
  92.1 1.0 %copy.22 = f32[32,16,512]{2,1,0:T(8,128)} copy(f32[32,16,512]{2,1,0:T(8,128)S(1)} %get-tuple-element.7) | data formatting | bytes 2097152
  (2 shorter events, 0.0 us)
Async XLA Ops:
  0.6 1.7 %copy-start.3 = (f32[16,512]{1,0:T(8,128)S(1)}, f32[16,512]{1,0:T(8,128)}, u32[]{:S(2)}) copy-start(f32[16,512]{1,0:T(8,128)} %param.8) | copy-start | bytes 98308
  0.6 3.1 %copy-start = (f32[32,16,512]{2,1,0:T(8,128)S(1)}, f32[32,16,512]{2,1,0:T(8,128)}, u32[]{:S(2)}) copy-start(f32[32,16,512]{2,1,0:T(8,128)} %params_ref.1) | copy-start | bytes 3145732
  3.6 0.7 copy-start.1
  3.6 0.7 copy-start.2
